TPU v7x, 32 devices: a whole 2x2x4 slice. The times are simulated.
32 devices in a mesh: grp: 2 (over x), dp: 16 (over z, y, core).
Axes of the slice: x: 2, y: 2, z: 4, core: 2. Of those that a mesh axis runs over, the one named last changes fastest.
Arguments:
- tokens_in: bfloat16 [8192, 1024], P(('grp', 'dp')), may hold values from -6 to 6
- grad_out: bfloat16 [8192, 1024], P(('grp', 'dp')), may hold values from -6 to 6
- seq_lengths: int32 [16, 16], P('dp'), may hold values from 1 to 125, as said below
- seq_deal: int32 [16, 16], P('dp'), may hold values from 0 to 15, as said below
- norm_attn: bfloat16 [1024], P(('grp', 'dp')), may hold values from 0.099609375 to 1.8984375
- query_key_value_weight: bfloat16 [1024, 4096], P(('grp', 'dp')), may hold values from -0.1875 to 0.1875
- query_norm_gain: bfloat16 [128], P(('grp', 'dp')), may hold values from 0.099609375 to 1.8984375
- k_gain: bfloat16 [128], P(('grp', 'dp')), may hold values from 0.099609375 to 1.8984375
- output_weight: bfloat16 [2048, 1024], P(('grp', 'dp')), may hold values from -0.375 to 0.375
- norm_mlp: bfloat16 [1024], P(('grp', 'dp')), may hold values from 0.099609375 to 1.8984375
- w_gate_up: bfloat16 [1024, 6144], P(('grp', 'dp')), may hold values from -0.1875 to 0.1875
- w_down: bfloat16 [3072, 1024], P(('grp', 'dp')), may hold values from -0.109375 to 0.109375
Outputs:
- y_out: bfloat16 [8192, 1024], P(('grp', 'dp'))
- grad_in: float32 [8192, 1024], P(('grp', 'dp'))
- grad_norm_attn: float32 [1024], P(('grp', 'dp'))
- grad_qkv: float32 [1024, 4096], P(('grp', 'dp'))
- grad_q_gain: float32 [128], P(('grp', 'dp'))
- grad_k_gain: float32 [128], P(('grp', 'dp'))
- grad_out_proj: float32 [2048, 1024], P(('grp', 'dp'))
- grad_norm_mlp: float32 [1024], P(('grp', 'dp'))
- grad_gate_up: float32 [1024, 6144], P(('grp', 'dp'))
- grad_down: float32 [3072, 1024], P(('grp', 'dp'))
Inputs may be any that keep to these rules, and one draw needn't show every extreme that they name: `seq_lengths`: each row sums to 512. `seq_deal`: each row is a permutation; for each grp index c and micro-batch m, the sequences in slots (c * 2 + m) * 4 + j, j below 4, have lengths that sum to 128.
All inputs are finite; a program needn't handle non-finite values.
Results may differ from a plain program's by a relative error of at most 0.015.
Values may be sent and summed in bfloat16 or wider, within the bound.
No kernel may reach another device: no remote copies, remote signals or barrier semaphores. Data moves between devices by JAX's collectives and lax.ppermute only.
A program may use at most 192 MiB of HBM per device.

v0:
```python
from functools import reduce

import jax
import jax.numpy as jnp
from jax import lax
from jax.sharding import PartitionSpec as P

QUERY_HEADS = 16
KEY_VALUE_HEADS = 8
HEAD_SIZE = 128
FF = 3072
MB_TOK = 128
SEQ_GROUP = 4


EPSILON = 1e-06
ROPE_BASE = 1000000.0
MASKED = -1e30


def swapped(x, axis, stride):
    return lax.ppermute(x, axis, [(i, i ^ 1 << stride) for i in range(lax.axis_size(axis))])


def deal_slots(lengths, deal_order):
    token_count = lengths.shape[0]
    seq_ids = jnp.arange(token_count, dtype=jnp.int32)
    starts = jnp.cumsum(lengths) - lengths
    pick = (deal_order[:, None] == seq_ids[None, :]).astype(jnp.int32)
    slot_length = jnp.sum(pick * lengths[None, :], axis=1)
    slot_source = jnp.sum(pick * starts[None, :], axis=1)
    groups = token_count // SEQ_GROUP
    grouped = slot_length.reshape(groups, SEQ_GROUP)
    offsets = jnp.cumsum(grouped, axis=1) - grouped
    slot_dealt = (offsets + jnp.arange(groups, dtype=jnp.int32)[:, None] * MB_TOK).reshape(
        token_count
    )
    return (seq_ids, starts, pick, slot_length, slot_source, slot_dealt)


def deal_rows(lengths, deal_order):
    seq_ids, starts, pick, slot_length, slot_source, slot_dealt = deal_slots(lengths, deal_order)
    total_rows = lengths.shape[0] // SEQ_GROUP * MB_TOK
    rows = jnp.arange(total_rows, dtype=jnp.int32)
    inside = (
        (rows[:, None] >= slot_dealt[None, :])
        & (rows[:, None] < (slot_dealt + slot_length)[None, :])
    ).astype(jnp.int32)
    source = rows + jnp.sum(inside * (slot_source - slot_dealt)[None, :], axis=1)
    segment = jnp.sum(inside * seq_ids[None, :], axis=1)
    position = rows - jnp.sum(inside * slot_dealt[None, :], axis=1)
    return (source, segment, position)


def back_rows(lengths, deal_order):
    seq_ids, starts, pick, slot_length, slot_source, slot_dealt = deal_slots(lengths, deal_order)
    seq_dealt = jnp.sum(pick * slot_dealt[:, None], axis=0)
    total_rows = lengths.shape[0] // SEQ_GROUP * MB_TOK
    rows = jnp.arange(total_rows, dtype=jnp.int32)
    inside = (
        (rows[:, None] >= starts[None, :]) & (rows[:, None] < (starts + lengths)[None, :])
    ).astype(jnp.int32)
    return rows + jnp.sum(inside * (seq_dealt - starts)[None, :], axis=1)


def root_mean_scale(values):
    return lax.rsqrt(jnp.mean(values * values, axis=-1, keepdims=True) + EPSILON)


def norm_back(grad_norm, inputs, scale, gain):
    weighted = grad_norm * gain
    return scale * weighted - inputs * (scale * scale * scale) * jnp.mean(
        weighted * inputs, axis=-1, keepdims=True
    )


def rope_tables(position):
    half_width = HEAD_SIZE // 2
    frequency = ROPE_BASE ** (-2.0 * jnp.arange(half_width, dtype=jnp.float32) / HEAD_SIZE)
    angles = position.astype(jnp.float32)[:, None] * frequency[None, :]
    cosine_table = jnp.concatenate([jnp.cos(angles), jnp.cos(angles)], axis=-1)[:, None, :]
    sine_table = jnp.concatenate([jnp.sin(angles), jnp.sin(angles)], axis=-1)[:, None, :]
    return (cosine_table, sine_table)


def apply_rotation(inputs, cosine_table, sine_table):
    half_width = inputs.shape[-1] // 2
    turned = jnp.concatenate([-inputs[..., half_width:], inputs[..., :half_width]], axis=-1)
    return inputs * cosine_table + turned * sine_table


def rotate_back(grads, cosine_table, sine_table):
    half_width = grads.shape[-1] // 2
    sined = grads * sine_table
    return grads * cosine_table + jnp.concatenate(
        [sined[..., half_width:], -sined[..., :half_width]], axis=-1
    )


def multiply_by_transpose(left, weight):
    return lax.dot_general(
        left, weight, (((1,), (1,)), ((), ())), preferred_element_type=jnp.float32
    )


def rows_product(left, right):
    return lax.dot_general(
        left, right, (((0,), (0,)), ((), ())), preferred_element_type=jnp.float32
    )


def attention_scores(query_reduced, key_low, allowed):
    scores = jnp.einsum(
        "tkgd,skd->kgts", query_reduced, key_low, preferred_element_type=jnp.float32
    ) * HEAD_SIZE ** (-0.5)
    return jnp.where(allowed[None, None], scores, MASKED)


def fetch_attention(norm_attn, query_key_value_weight, query_norm_gain, k_gain, output_weight):
    return (
        lax.all_gather(norm_attn, ("grp", "dp"), axis=0, tiled=True),
        lax.all_gather(query_key_value_weight, ("grp", "dp"), axis=0, tiled=True),
        lax.all_gather(query_norm_gain, ("grp", "dp"), axis=0, tiled=True),
        lax.all_gather(k_gain, ("grp", "dp"), axis=0, tiled=True),
        lax.all_gather(output_weight, ("grp", "dp"), axis=0, tiled=True),
    )


def fetch_feedforward(norm_mlp, w_gate_up, w_down):
    return (
        lax.all_gather(norm_mlp, ("grp", "dp"), axis=0, tiled=True),
        lax.all_gather(w_gate_up, ("grp", "dp"), axis=0, tiled=True),
        lax.all_gather(w_down, ("grp", "dp"), axis=0, tiled=True),
    )


def forward_block(x_rows, segment, position, attn_weights, ffn_weights):
    norm_one, query_key_value_weight, query_norm_gain, k_gain, output_weight = attn_weights
    norm_two, w_gate_up, w_down = ffn_weights
    token_count = x_rows.shape[0]
    query_width = QUERY_HEADS * HEAD_SIZE
    key_value_width = KEY_VALUE_HEADS * HEAD_SIZE
    x_float = x_rows.astype(jnp.float32)
    scale_one = root_mean_scale(x_float)
    normed_one = (x_float * scale_one * norm_one.astype(jnp.float32)).astype(jnp.bfloat16)
    projected_output = jnp.dot(
        normed_one, query_key_value_weight, preferred_element_type=jnp.float32
    )
    query_rows = projected_output[:, :query_width].reshape(token_count, QUERY_HEADS, HEAD_SIZE)
    unnormed_keys = projected_output[:, query_width : query_width + key_value_width].reshape(
        token_count, KEY_VALUE_HEADS, HEAD_SIZE
    )
    value_reduced = (
        projected_output[:, query_width + key_value_width :]
        .astype(jnp.bfloat16)
        .reshape(token_count, KEY_VALUE_HEADS, HEAD_SIZE)
    )
    scale_q = root_mean_scale(query_rows)
    scale_k = root_mean_scale(unnormed_keys)
    cosine_table, sine_table = rope_tables(position)
    query_reduced = (
        apply_rotation(
            query_rows * scale_q * query_norm_gain.astype(jnp.float32), cosine_table, sine_table
        )
        .astype(jnp.bfloat16)
        .reshape(token_count, KEY_VALUE_HEADS, QUERY_HEADS // KEY_VALUE_HEADS, HEAD_SIZE)
    )
    key_low = apply_rotation(
        unnormed_keys * scale_k * k_gain.astype(jnp.float32), cosine_table, sine_table
    ).astype(jnp.bfloat16)
    allowed = (segment[:, None] == segment[None, :]) & (position[None, :] <= position[:, None])
    scores = attention_scores(query_reduced, key_low, allowed)
    top_score = jnp.max(scores, axis=-1, keepdims=True)
    expo = jnp.exp(scores - top_score)
    total = jnp.sum(expo, axis=-1, keepdims=True)
    probs = expo / total
    log_total = top_score[..., 0] + jnp.log(total[..., 0])
    attended = (
        jnp.einsum(
            "kgts,skd->tkgd",
            probs.astype(jnp.bfloat16),
            value_reduced,
            preferred_element_type=jnp.float32,
        )
        .reshape(token_count, query_width)
        .astype(jnp.bfloat16)
    )
    residual = x_float + jnp.dot(attended, output_weight, preferred_element_type=jnp.float32)
    scale_two = root_mean_scale(residual)
    normed_two = (residual * scale_two * norm_two.astype(jnp.float32)).astype(jnp.bfloat16)
    gate_up = jnp.dot(normed_two, w_gate_up, preferred_element_type=jnp.float32)
    activated = (jax.nn.silu(gate_up[:, :FF]) * gate_up[:, FF:]).astype(jnp.bfloat16)
    output = residual + jnp.dot(activated, w_down, preferred_element_type=jnp.float32)
    saved = (
        x_float,
        scale_one,
        normed_one,
        query_rows,
        unnormed_keys,
        scale_q,
        scale_k,
        query_reduced,
        key_low,
        value_reduced,
        allowed,
        log_total,
        attended,
        residual,
        scale_two,
        normed_two,
        gate_up,
        activated,
        cosine_table,
        sine_table,
    )
    return (output, saved)


def backward_block(grad_rows, saved, attn_weights, ffn_weights):
    norm_one, query_key_value_weight, query_norm_gain, k_gain, output_weight = attn_weights
    norm_two, w_gate_up, w_down = ffn_weights
    (
        x_float,
        scale_one,
        normed_one,
        query_rows,
        unnormed_keys,
        scale_q,
        scale_k,
        query_reduced,
        key_low,
        value_reduced,
        allowed,
        log_total,
        attended,
        residual,
        scale_two,
        normed_two,
        gate_up,
        activated,
        cosine_table,
        sine_table,
    ) = saved
    token_count = grad_rows.shape[0]
    query_width = QUERY_HEADS * HEAD_SIZE
    key_value_width = KEY_VALUE_HEADS * HEAD_SIZE
    grad_float = grad_rows.astype(jnp.float32)
    grad_act = multiply_by_transpose(grad_rows, w_down)
    gate = gate_up[:, :FF]
    up_part = gate_up[:, FF:]
    sigmoid = jax.nn.sigmoid(gate)
    grad_gate = grad_act * up_part * (sigmoid * (1.0 + gate * (1.0 - sigmoid)))
    grad_up = grad_act * (gate * sigmoid)
    grad_gate_up = jnp.concatenate([grad_gate, grad_up], axis=1).astype(jnp.bfloat16)
    grad_normed_two = multiply_by_transpose(grad_gate_up, w_gate_up)
    gain_two = norm_two.astype(jnp.float32)
    term_norm_two = jnp.sum(grad_normed_two * residual * scale_two, axis=0)
    grad_residual = grad_float + norm_back(grad_normed_two, residual, scale_two, gain_two)
    branch_gradient = grad_residual.astype(jnp.bfloat16)
    grad_attended = (
        multiply_by_transpose(branch_gradient, output_weight)
        .astype(jnp.bfloat16)
        .reshape(token_count, KEY_VALUE_HEADS, QUERY_HEADS // KEY_VALUE_HEADS, HEAD_SIZE)
    )
    scores = attention_scores(query_reduced, key_low, allowed)
    probs = jnp.exp(scores - log_total[..., None])
    grad_probs = jnp.einsum(
        "tkgd,skd->kgts", grad_attended, value_reduced, preferred_element_type=jnp.float32
    )
    grad_scores = (
        probs * (grad_probs - jnp.sum(probs * grad_probs, axis=-1, keepdims=True))
    ).astype(jnp.bfloat16)
    grad_query = jnp.einsum(
        "kgts,skd->tkgd", grad_scores, key_low, preferred_element_type=jnp.float32
    ) * HEAD_SIZE ** (-0.5)
    grad_key = jnp.einsum(
        "kgts,tkgd->skd", grad_scores, query_reduced, preferred_element_type=jnp.float32
    ) * HEAD_SIZE ** (-0.5)
    grad_value = jnp.einsum(
        "kgts,tkgd->skd",
        probs.astype(jnp.bfloat16),
        grad_attended,
        preferred_element_type=jnp.float32,
    )
    grad_qn = rotate_back(
        grad_query.reshape(token_count, QUERY_HEADS, HEAD_SIZE), cosine_table, sine_table
    )
    grad_kn = rotate_back(grad_key, cosine_table, sine_table)
    term_q = jnp.sum(grad_qn * query_rows * scale_q, axis=(0, 1))
    term_k = jnp.sum(grad_kn * unnormed_keys * scale_k, axis=(0, 1))
    grad_q_raw = norm_back(grad_qn, query_rows, scale_q, query_norm_gain.astype(jnp.float32))
    grad_k_raw = norm_back(grad_kn, unnormed_keys, scale_k, k_gain.astype(jnp.float32))
    grad_projected = jnp.concatenate(
        [
            grad_q_raw.reshape(token_count, query_width),
            grad_k_raw.reshape(token_count, key_value_width),
            grad_value.reshape(token_count, key_value_width),
        ],
        axis=1,
    ).astype(jnp.bfloat16)
    grad_normed_one = multiply_by_transpose(grad_projected, query_key_value_weight)
    gain_one = norm_one.astype(jnp.float32)
    term_norm_one = jnp.sum(grad_normed_one * x_float * scale_one, axis=0)
    grad_input = grad_residual + norm_back(grad_normed_one, x_float, scale_one, gain_one)
    products = (
        normed_one,
        grad_projected,
        attended,
        branch_gradient,
        normed_two,
        grad_gate_up,
        activated,
        grad_rows,
    )
    gains = (term_norm_one, term_q, term_k, term_norm_two)
    return (grad_input, products, gains)


def weight_terms(products):
    return (
        rows_product(products[0], products[1]),
        rows_product(products[2], products[3]),
        rows_product(products[4], products[5]),
        rows_product(products[6], products[7]),
    )


def add_trees(first_tree, second_tree):
    return jax.tree.map(jnp.add, first_tree, second_tree)


def on_device(
    tokens_in,
    grad_out,
    seq_lengths,
    seq_deal,
    norm_attn,
    query_key_value_weight,
    query_norm_gain,
    k_gain,
    output_weight,
    norm_mlp,
    w_gate_up,
    w_down,
):
    tok_dev = tokens_in.shape[0]
    grp_side = lax.axis_index("grp")
    first_row = grp_side * tok_dev
    source, segment, position = deal_rows(seq_lengths[0], seq_deal[0])
    own_source = lax.dynamic_slice_in_dim(source, first_row, tok_dev)
    own_segment = lax.dynamic_slice_in_dim(segment, first_row, tok_dev)
    own_position = lax.dynamic_slice_in_dim(position, first_row, tok_dev)
    peer_tokens = swapped(tokens_in, "grp", 0)
    paired = jnp.where(
        grp_side == 0,
        jnp.concatenate([tokens_in, peer_tokens], axis=0),
        jnp.concatenate([peer_tokens, tokens_in], axis=0),
    )
    dealt_tokens = jnp.take(paired, own_source, axis=0)
    micro_count = tok_dev // MB_TOK
    output_list = []
    grad_list = []
    kept_list = []
    gain_list = []
    for micro_step in range(micro_count):
        row_start = micro_step * MB_TOK
        row_stop = row_start + MB_TOK
        attn_weights = fetch_attention(
            norm_attn, query_key_value_weight, query_norm_gain, k_gain, output_weight
        )
        ffn_weights = fetch_feedforward(norm_mlp, w_gate_up, w_down)
        output, saved = forward_block(
            dealt_tokens[row_start:row_stop],
            own_segment[row_start:row_stop],
            own_position[row_start:row_stop],
            attn_weights,
            ffn_weights,
        )
        output_list.append(output)
        back_ffn = fetch_feedforward(norm_mlp, w_gate_up, w_down)
        back_attn = fetch_attention(
            norm_attn, query_key_value_weight, query_norm_gain, k_gain, output_weight
        )
        grad_input, products, gains = backward_block(
            grad_out[row_start:row_stop], saved, back_attn, back_ffn
        )
        grad_list.append(grad_input)
        kept_list.append(products)
        gain_list.append(gains)
    joined = tuple(
        (jnp.concatenate([kept[index] for kept in kept_list], axis=0) for index in range(8))
    )
    terms = weight_terms(joined)
    gain_sums = reduce(add_trees, gain_list)
    owned = (
        lax.psum_scatter(gain_sums[0], ("grp", "dp"), scatter_dimension=0, tiled=True),
        lax.psum_scatter(terms[0], ("grp", "dp"), scatter_dimension=0, tiled=True),
        lax.psum_scatter(gain_sums[1], ("grp", "dp"), scatter_dimension=0, tiled=True),
        lax.psum_scatter(gain_sums[2], ("grp", "dp"), scatter_dimension=0, tiled=True),
        lax.psum_scatter(terms[1], ("grp", "dp"), scatter_dimension=0, tiled=True),
        lax.psum_scatter(gain_sums[3], ("grp", "dp"), scatter_dimension=0, tiled=True),
        lax.psum_scatter(terms[2], ("grp", "dp"), scatter_dimension=0, tiled=True),
        lax.psum_scatter(terms[3], ("grp", "dp"), scatter_dimension=0, tiled=True),
    )
    y_out = jnp.concatenate(output_list, axis=0).astype(jnp.bfloat16)
    grad_dealt = jnp.concatenate(grad_list, axis=0)
    peer_grads = swapped(grad_dealt.astype(jnp.bfloat16), "grp", 0).astype(grad_dealt.dtype)
    paired_grads = jnp.where(
        grp_side == 0,
        jnp.concatenate([grad_dealt, peer_grads], axis=0),
        jnp.concatenate([peer_grads, grad_dealt], axis=0),
    )
    target = back_rows(seq_lengths[0], seq_deal[0])
    own_target = lax.dynamic_slice_in_dim(target, first_row, tok_dev)
    grad_in = jnp.take(paired_grads, own_target, axis=0)
    return (
        y_out,
        grad_in,
        owned[0],
        owned[1],
        owned[2],
        owned[3],
        owned[4],
        owned[5],
        owned[6],
        owned[7],
    )


def solution(mesh):
    in_specs = (
        P(("grp", "dp"), None),
        P(("grp", "dp"), None),
        P("dp", None),
        P("dp", None),
        P(("grp", "dp")),
        P(("grp", "dp"), None),
        P(("grp", "dp")),
        P(("grp", "dp")),
        P(("grp", "dp"), None),
        P(("grp", "dp")),
        P(("grp", "dp"), None),
        P(("grp", "dp"), None),
    )
    out_specs = (
        P(("grp", "dp"), None),
        P(("grp", "dp"), None),
        P(("grp", "dp")),
        P(("grp", "dp"), None),
        P(("grp", "dp")),
        P(("grp", "dp")),
        P(("grp", "dp"), None),
        P(("grp", "dp")),
        P(("grp", "dp"), None),
        P(("grp", "dp"), None),
    )
    return jax.shard_map(
        on_device, mesh=mesh, in_specs=in_specs, out_specs=out_specs, check_vma=False
    )
```

profile of v0, /device:TPU:1, one launch (start us, length us, event | category | flops | bytes accessed | tf_op | source)
XLA Modules:
  0.0 1117.6 jit_solution(1043521751701661519)
XLA Ops:
  15.0 45.1 %all-reduce.9 = (bf16[1024]{0:T(1024)(128)(2,1)S(1)}, bf16[128]{0:T(256)(128)(2,1)S(1)}, bf16[128]{0:T(256)(128)(2,1)S(1)}, bf16[1024]{0:T(1024)(128)(2,1)S(1)}) all-reduce(bf16[1024]{0:T(1024)(128)(2,1)S(1)} %dynamic-update-slice, bf16[128]{0:T(256)(128)(2,1)S(1)} %dynamic-update-slice.1, ...), channel_id=1, replica_groups=mesh['grp'=2,'dp'=16] {'grp','dp'}, use_global_device_ids=true, to_apply=%add | all-reduce | flops 2304 | bytes 9216
  75.1 16.7 %all-gather.5.cloned.1.call-done = bf16[1024,4096]{1,0:T(8,128)(2,1)} async-done(((bf16[32,4096]{1,0:T(8,128)(2,1)}), bf16[1024,4096]{1,0:T(8,128)(2,1)}) %all-gather.5.cloned.1.call-update) | async-done | bytes 8388624 | tf_op jit(solution)/shard_map/all_gather | solution.py:122
  91.7 4.6 fusion.152
  98.4 4.7 fusion.154
  120.3 35.2 %all-gather.7.cloned.1.call-done = bf16[2048,1024]{1,0:T(8,128)(2,1)} async-done(((bf16[64,1024]{1,0:T(8,128)(2,1)}), bf16[2048,1024]{1,0:T(8,128)(2,1)}) %all-gather.7.cloned.1.call-update) | async-done | bytes 4194320 | tf_op jit(solution)/shard_map/all_gather | solution.py:125
  163.4 89.5 %all-gather.9.cloned.1.call-done = bf16[1024,6144]{1,0:T(8,128)(2,1)} async-done(((bf16[32,6144]{1,0:T(8,128)(2,1)}), bf16[1024,6144]{1,0:T(8,128)(2,1)}) %all-gather.9.cloned.1.call-update) | async-done | bytes 12582928 | tf_op jit(solution)/shard_map/all_gather | solution.py:132
  252.9 8.5 fusion.153
  261.4 62.1 %all-gather.11.cloned.1.call-done = bf16[3072,1024]{1,0:T(8,128)(2,1)} async-done(((bf16[96,1024]{1,0:T(8,128)(2,1)}), bf16[3072,1024]{1,0:T(8,128)(2,1)}) %all-gather.11.cloned.1.call-update) | async-done | bytes 6291472 | tf_op jit(solution)/shard_map/all_gather | solution.py:133
  323.5 7.7 multiply_convert_fusion.3
  331.2 7.5 multiply_reduce_fusion.7
  342.1 6.8 multiply_convert_fusion.1
  349.0 7.4 multiply_reduce_fusion.6
  360.1 4.5 fusion.62
  366.2 6.4 fusion.28
  385.6 3.8 convolution_convert_fusion.1
  421.6 14.3 %fusion.8 = f32[1024,4096]{1,0:T(8,128)} fusion(bf16[128,1024]{1,0:T(8,128)(2,1)S(1)} %copy-done.65, bf16[128,1024]{1,0:T(8,128)(2,1)S(1)} %copy-done.67, bf16[128,2048]{1,0:T(8,128)(2,1)S(1)} %get-tuple-element.58, bf16[128,1024]{1,0:T(8,128)(2,1)S(1)} %copy-done.69, bf16[128,1024]{1,0:T(8,128)(2,1)S(1)} %copy-done.71, ...), kind=kOutput, calls=%fused_computation.13 | convolution fusion | flops 2161115136 | bytes 19398656 | tf_op jit(solution)/shard_map/dot_general | solution.py:107
  437.8 18.0 %fusion = f32[1024,6144]{1,0:T(8,128)} fusion(bf16[128,3072]{1,0:T(8,128)(2,1)S(1)} %copy-done.40, bf16[128,3072]{1,0:T(8,128)(2,1)S(1)} %copy-done.39, bf16[128,3072]{1,0:T(8,128)(2,1)S(1)} %copy-done.38, bf16[128,3072]{1,0:T(8,128)(2,1)S(1)} %copy-done.37, bf16[128,1024]{1,0:T(8,128)(2,1)S(1)} %copy-done.45, bf16[128,1024]{1,0:T(8,128)(2,1)} %copy-done.46), kind=kOutput, calls=%fused_computation.2 | convolution fusion | flops 3234856960 | bytes 28835840 | tf_op jit(solution)/shard_map/dot_general | solution.py:107
  457.1 6.5 fusion.56
  463.7 6.5 fusion.88
  473.7 51.0 %all-reduce.8 = (f32[1024]{0:T(1024)S(1)}, f32[128]{0:T(128)S(1)}, f32[128]{0:T(128)S(1)}, f32[1024]{0:T(1024)S(1)}) all-reduce(f32[1024]{0:T(1024)S(1)} %add.315, f32[128]{0:T(128)S(1)} %add.316, f32[128]{0:T(128)S(1)} %add.317, f32[1024]{0:T(1024)S(1)} %add.318), channel_id=2, replica_groups=mesh['grp'=2,'dp'=16] {'grp','dp'}, use_global_device_ids=true, to_apply=%region_33.34.clone | all-reduce | flops 2304 | bytes 18432
  527.1 4.3 fusion.39
  537.5 131.7 %reduce-scatter.11.cloned.1.call-done = f32[96,1024]{1,0:T(8,128)} async-done(((f32[3072,1024]{1,0:T(8,128)}), f32[96,1024]{1,0:T(8,128)}) %reduce-scatter.11.cloned.1.call-update) | async-done | bytes 393232 | tf_op jit(solution)/shard_map/reduce_scatter | solution.py:403
  669.2 187.4 %reduce-scatter.5.cloned.1.call-done = f32[32,4096]{1,0:T(8,128)} async-done(((f32[1024,4096]{1,0:T(8,128)}), f32[32,4096]{1,0:T(8,128)}) %reduce-scatter.5.cloned.1.call-update) | async-done | bytes 524304 | tf_op jit(solution)/shard_map/reduce_scatter | solution.py:397
  856.5 254.0 %reduce-scatter.9.cloned.1.call-done = f32[32,6144]{1,0:T(8,128)} async-done(((f32[1024,6144]{1,0:T(8,128)}), f32[32,6144]{1,0:T(8,128)}) %reduce-scatter.9.cloned.1.call-update) | async-done | bytes 786448 | tf_op jit(solution)/shard_map/reduce_scatter | solution.py:402
  (476 shorter events, 117.2 us)
Async XLA Ops:
  7.2 84.6 %all-gather.5.cloned.1.call-start = ((), (), s32[]{:S(2)}) async-start(), calls=%async_computation.4 | async-start | bytes 8650752 | tf_op jit(solution)/shard_map/all_gather | solution.py:122
  7.9 147.5 %all-gather.7.cloned.1.call-start = ((), (), s32[]{:S(2)}) async-start(), calls=%async_computation.5 | async-start | bytes 4325376 | tf_op jit(solution)/shard_map/all_gather | solution.py:125
  8.7 244.3 %all-gather.9.cloned.1.call-start = ((), (), s32[]{:S(2)}) async-start(), calls=%async_computation.6 | async-start | bytes 12976128 | tf_op jit(solution)/shard_map/all_gather | solution.py:132
  9.4 314.1 %all-gather.11.cloned.1.call-start = ((), (), s32[]{:S(2)}) async-start(), calls=%async_computation.7 | async-start | bytes 6488064 | tf_op jit(solution)/shard_map/all_gather | solution.py:133
  9.4 61.2 %collective-permute-start = (bf16[256,1024]{1,0:T(8,128)(2,1)}, bf16[256,1024]{1,0:T(8,128)(2,1)S(1)}, u32[]{:S(2)}, u32[]{:S(2)}) collective-permute-start(bf16[256,1024]{1,0:T(8,128)(2,1)} %param.12), channel_id=1, source_target_pairs={{0,16},{16,0},{1,17},{17,1},{2,18},{18,2},{3,19},{19,3},{4,20},{20... | collective-permute-start | bytes 1572872 | tf_op jit(solution)/shard_map/ppermute | solution.py:22
  11.6 525.9 %reduce-scatter.7.cloned.1.call-start = ((), (), s32[]{:S(2)}) async-start(), calls=%async_computation.9 | async-start | bytes 8650752 | tf_op jit(solution)/shard_map/reduce_scatter | solution.py:400
  73.6 85.9 %copy-start.10 = (bf16[256,1024]{1,0:T(8,128)(2,1)}, bf16[256,1024]{1,0:T(8,128)(2,1)S(1)}, u32[]{:S(2)}) copy-start(bf16[256,1024]{1,0:T(8,128)(2,1)S(1)} %broadcast_select_fusion.1) | copy-start | bytes 1572868
  74.3 22.1 %copy-start.124 = (f32[128]{0:T(128)}, f32[128]{0:T(128)S(1)}, u32[]{:S(2)}) copy-start(f32[128]{0:T(128)S(1)} %get-tuple-element.119) | copy-start | bytes 1540
  75.1 23.3 %copy-start.35 = (bf16[128,1024]{1,0:T(8,128)(2,1)}, bf16[128,1024]{1,0:T(8,128)(2,1)S(1)}, u32[]{:S(2)}) copy-start(bf16[128,1024]{1,0:T(8,128)(2,1)S(1)} %get-tuple-element.82) | copy-start | bytes 786436
  117.3 41.8 %copy-start.8 = (f32[8,2,128,128]{2,3,1,0:T(8,128)}, f32[8,2,128,128]{2,3,1,0:T(8,128)S(1)}, u32[]{:S(2)}) copy-start(f32[8,2,128,128]{2,3,1,0:T(8,128)S(1)} %get-tuple-element.140) | copy-start | bytes 3145732
  118.8 39.7 %copy-start.92 = (f32[8,2,128]{2,1,0:T(2,128)}, f32[8,2,128]{2,1,0:T(2,128)S(1)}, u32[]{:S(2)}) copy-start(f32[8,2,128]{2,1,0:T(2,128)S(1)} %get-tuple-element.141) | copy-start | bytes 24580
  119.0 39.5 %copy-start.105 = (f32[8,2,128]{2,1,0:T(2,128)}, f32[8,2,128]{2,1,0:T(2,128)S(1)}, u32[]{:S(2)}) copy-start(f32[8,2,128]{2,1,0:T(2,128)S(1)} %fusion.74) | copy-start | bytes 24580
  120.2 39.2 %copy-start.57 = (bf16[8,128,2,128]{3,1,2,0:T(8,128)(2,1)}, bf16[8,128,2,128]{3,1,2,0:T(8,128)(2,1)S(1)}, u32[]{:S(2)}) copy-start(bf16[8,128,2,128]{3,1,2,0:T(8,128)(2,1)S(1)} %convolution_convert_fusion.3) | copy-start | bytes 1572868
  163.4 98.0 %copy-start.46 = (bf16[128,1024]{1,0:T(8,128)(2,1)}, bf16[128,1024]{1,0:T(8,128)(2,1)S(1)}, u32[]{:S(2)}) copy-start(bf16[128,1024]{1,0:T(8,128)(2,1)S(1)} %multiply_convert_fusion.9) | copy-start | bytes 786436
  261.4 69.8 %copy-start.88 = (f32[1024]{0:T(1024)S(1)}, f32[1024]{0:T(1024)}, u32[]{:S(2)}) copy-start(f32[1024]{0:T(1024)} %convert_element_type.149) | copy-start | bytes 12292
  261.4 69.8 %copy-start.117 = (f32[128]{0:T(128)S(1)}, f32[128]{0:T(128)}, u32[]{:S(2)}) copy-start(f32[128]{0:T(128)} %get-tuple-element.130) | copy-start | bytes 1540
  261.4 69.8 %copy-start.121 = (f32[128]{0:T(128)S(1)}, f32[128]{0:T(128)}, u32[]{:S(2)}) copy-start(f32[128]{0:T(128)} %copy-done.120) | copy-start | bytes 1540
  364.7 304.5 %reduce-scatter.11.cloned.1.call-start = ((), (), s32[]{:S(2)}) async-start(), calls=%async_computation.11 | async-start | bytes 12976128 | tf_op jit(solution)/shard_map/reduce_scatter | solution.py:403
  372.6 483.9 %reduce-scatter.5.cloned.1.call-start = ((), (), s32[]{:S(2)}) async-start(), calls=%async_computation.8 | async-start | bytes 17301504 | tf_op jit(solution)/shard_map/reduce_scatter | solution.py:397
  435.9 674.7 %reduce-scatter.9.cloned.1.call-start = ((), (), s32[]{:S(2)}) async-start(), calls=%async_computation.10 | async-start | bytes 25952256 | tf_op jit(solution)/shard_map/reduce_scatter | solution.py:402
  470.2 56.8 %copy-start.14 = (f32[128,1024]{1,0:T(8,128)S(1)}, f32[128,1024]{1,0:T(8,128)}, u32[]{:S(2)}) copy-start(f32[128,1024]{1,0:T(8,128)} %get-tuple-element.146) | copy-start | bytes 1572868
  470.2 56.8 %copy-start.44 = (bf16[128,3072]{1,0:T(8,128)(2,1)S(1)}, bf16[128,3072]{1,0:T(8,128)(2,1)}, u32[]{:S(2)}) copy-start(bf16[128,3072]{1,0:T(8,128)(2,1)} %get-tuple-element.66) | copy-start | bytes 2359300
  470.3 61.1 %slice-start = ((s8[6291456]{0:T(1024)(128)(4,1)}), s8[2097152]{0:T(1024)(128)(4,1)S(1)}, s32[]{:S(2)}) async-start(s8[6291456]{0:T(1024)(128)(4,1)} %bitcast.230), calls=%async_computation.12 | async-start | bytes 4194304
  472.5 61.5 %collective-permute-start.1 = (bf16[256,1024]{1,0:T(8,128)(2,1)}, bf16[256,1024]{1,0:T(8,128)(2,1)}, u32[]{:S(2)}, u32[]{:S(2)}) collective-permute-start(bf16[256,1024]{1,0:T(8,128)(2,1)} %pad_maximum_fusion.3), channel_id=1, source_target_pairs={{0,16},{16,0},{1,17},{17,1},{2,18},{18,2},{3,19},{19,3},{4,20},{20... | collective-permute-start | bytes 1572872 | tf_op jit(solution)/shard_map/ppermute | solution.py:22
  (125 other events, 448.0 us)
Sparse Core Ops, SparseCore 0:
  10.9 80.8 all-gather.4
  94.6 60.7 all-gather.6
  158.3 94.5 all-gather.8
  255.7 67.8 all-gather.10
  364.8 141.7 reduce-scatter.6
  513.1 156.0 reduce-scatter.10
  672.1 184.3 reduce-scatter.4
  864.7 245.8 reduce-scatter.8
where the time goes:
time: 1130 us; the launch traced here: 1120 us
  waiting for transfers between devices  779 us (69%)
  matrix products  130 us (12%)
  blocking collectives  96.1 us (9%)
  local copies, waits for them, and re-layouts  53.4 us (5%)
  other arithmetic  39.4 us (3%)
  between operations  16.3 us (1%)
    reduce_scatter x1, waiting for transfers between devices, on_device(): lax.psum_scatter(terms[2], ('grp', 'dp'), scatter_dimension=0, tiled=True)  254 us
    reduce_scatter x1, waiting for transfers between devices, on_device(): lax.psum_scatter(terms[0], ('grp', 'dp'), scatter_dimension=0, tiled=True)  187 us
    reduce_scatter x1, waiting for transfers between devices, on_device(): lax.psum_scatter(terms[3], ('grp', 'dp'), scatter_dimension=0, tiled=True)  132 us
    unnamed x2, blocking collectives  96.1 us
    all_gather x1, waiting for transfers between devices, fetch_feedforward(): lax.all_gather(w_gate_up, ('grp', 'dp'), axis=0, tiled=True)  89.5 us
    all_gather x1, waiting for transfers between devices, fetch_feedforward(): lax.all_gather(w_down, ('grp', 'dp'), axis=0, tiled=True)  62.1 us
    dot_general x8, matrix products, multiply_by_transpose(): lax.dot_general(left, weight, (((1,), (1,)), ((), ())), preferred_element...  49.9 us
    dot_general x4, matrix products, rows_product(): lax.dot_general(left, right, (((0,), (0,)), ((), ())), preferred_element_...  43.2 us
  transfers between devices with their start and end apart: 10, of which 7 were waited for; matrix products, arithmetic and copies ran while one was open for 15% of the time, Pallas kernels for 0%

commit v1 on v0

v1 whole, which is shorter than its diff:
```python
import jax
import jax.numpy as jnp
from jax import lax
from jax.experimental import pallas as pl
from jax.experimental.pallas import tpu as pltpu
from jax.sharding import PartitionSpec as P

QUERY_HEADS = 16
KEY_VALUE_HEADS = 8
HEAD_SIZE = 128
FF = 3072
MB_TOK = 128
SEQ_GROUP = 4

EPSILON = 1e-06
ROPE_BASE = 1000000.0
MASKED = -1e30
SCALE = HEAD_SIZE**-0.5
QUERIES_PER_KEY = QUERY_HEADS // KEY_VALUE_HEADS

BF16 = jnp.bfloat16
F32 = jnp.float32


def deal_slots(lengths, deal_order):
    token_count = lengths.shape[0]
    seq_ids = jnp.arange(token_count, dtype=jnp.int32)
    starts = jnp.cumsum(lengths) - lengths
    pick = (deal_order[:, None] == seq_ids[None, :]).astype(jnp.int32)
    slot_length = jnp.sum(pick * lengths[None, :], axis=1)
    slot_source = jnp.sum(pick * starts[None, :], axis=1)
    groups = token_count // SEQ_GROUP
    grouped = slot_length.reshape(groups, SEQ_GROUP)
    offsets = jnp.cumsum(grouped, axis=1) - grouped
    slot_dealt = (offsets + jnp.arange(groups, dtype=jnp.int32)[:, None] * MB_TOK).reshape(
        token_count
    )
    return (seq_ids, starts, pick, slot_length, slot_source, slot_dealt)


def deal_rows(lengths, deal_order, rows):
    _, _, _, slot_length, slot_source, slot_dealt = deal_slots(lengths, deal_order)
    inside = (
        (rows[:, None] >= slot_dealt[None, :])
        & (rows[:, None] < (slot_dealt + slot_length)[None, :])
    ).astype(jnp.int32)
    source = rows + jnp.sum(inside * (slot_source - slot_dealt)[None, :], axis=1)
    position = rows - jnp.sum(inside * slot_dealt[None, :], axis=1)
    return (source, position)


def back_rows(lengths, deal_order, rows):
    _, starts, pick, _, _, slot_dealt = deal_slots(lengths, deal_order)
    seq_dealt = jnp.sum(pick * slot_dealt[:, None], axis=0)
    inside = (
        (rows[:, None] >= starts[None, :]) & (rows[:, None] < (starts + lengths)[None, :])
    ).astype(jnp.int32)
    return rows + jnp.sum(inside * (seq_dealt - starts)[None, :], axis=1)


def take_rows(own, peer, rows, first_row):
    half = own.shape[0]
    near = jnp.remainder(rows - first_row, 2 * half)
    lane = lax.broadcasted_iota(jnp.int32, (rows.shape[0], half), 1)
    pick_own = (near[:, None] == lane).astype(own.dtype)
    pick_peer = (near[:, None] == lane + half).astype(own.dtype)
    return jnp.dot(pick_own, own, preferred_element_type=F32) + jnp.dot(
        pick_peer, peer, preferred_element_type=F32
    )


def swap(values, axis, mask):
    size = lax.axis_size(axis)
    return lax.ppermute(values, axis, [(i, i ^ mask) for i in range(size)])


def swap_core(values):
    return swap(values, "dp", 1)


def swap_y(values):
    return swap(values, "dp", 2)


def swap_z(values, step):
    return swap(values, "dp", 4 * step)


def swap_x(values):
    return swap(values, "grp", 1)


class Place:
    def __init__(self):
        index = lax.axis_index("dp")
        self.x = lax.axis_index("grp")
        self.core = index % 2
        self.y = (index // 2) % 2
        self.z = index // 4
        self.depth = lax.axis_size("dp") // 4
        self.chips = lax.axis_size("dp")


def ordered(bit, own, peer, axis):
    return jnp.where(
        bit == 0,
        jnp.concatenate([own, peer], axis=axis),
        jnp.concatenate([peer, own], axis=axis),
    )


def pick(values, index, axis):
    return lax.dynamic_index_in_dim(values, index, axis, keepdims=False)


def paired(bit, own, peer, axis):
    return ordered(bit, jnp.expand_dims(own, axis), jnp.expand_dims(peer, axis), axis)


def by_z(place, pieces, axis):
    step = 1
    groups = [jnp.expand_dims(piece, axis) for piece in pieces]
    while step < place.depth:
        bit = (place.z // step) % 2
        groups = [
            ordered(bit, groups[2 * i], groups[2 * i + 1], axis) for i in range(len(groups) // 2)
        ]
        step *= 2
    return groups[0]


def spread_z(place, piece, axis):
    pieces = [piece] + [swap_z(piece, step) for step in range(1, place.depth)]
    return by_z(place, pieces, axis)


def gather_late_x(place, stack):
    stack = paired(place.y, stack, swap_y(stack), 1)
    stack = paired(place.x, stack, swap_x(stack), 0)
    return stack.reshape(-1, stack.shape[-1])


def gather_late_y(place, stack):
    stack = paired(place.x, stack, swap_x(stack), 0)
    stack = paired(place.y, stack, swap_y(stack), 2)
    return stack.reshape(-1, stack.shape[-1])


def gather_halves(place, piece):
    half = piece.shape[1] // 2
    stack = spread_z(place, piece, 0)
    return (
        gather_late_x(place, stack[..., :half]),
        gather_late_y(place, stack[..., half:]),
    )


def gather_late_z(place, piece):
    half = piece.shape[1] // 2
    first, second = piece[:, :half], piece[:, half:]
    first = paired(place.x, first, swap_x(first), 0)
    first = paired(place.y, first, swap_y(first), 1)
    second = paired(place.y, second, swap_y(second), 0)
    second = paired(place.x, second, swap_x(second), 0)
    both = jnp.concatenate([first, second], axis=-1)
    stack = spread_z(place, both, 1)
    return stack.reshape(-1, stack.shape[-1])


def add(first, second):
    return (first.astype(F32) + second.astype(F32)).astype(BF16)


def scatter_plane(place, grads, first):
    depth = place.depth
    rows = grads.shape[0] // (4 * depth)
    grads = grads.reshape(2, depth, 2, rows, grads.shape[1])
    if first == "x":
        part = add(pick(grads, place.x, 0), swap_x(pick(grads, 1 - place.x, 0)))
        return add(pick(part, place.y, 1), swap_y(pick(part, 1 - place.y, 1)))
    part = add(pick(grads, place.y, 2), swap_y(pick(grads, 1 - place.y, 2)))
    return add(pick(part, place.x, 0), swap_x(pick(part, 1 - place.x, 0)))


def scatter_z(place, part):
    total = pick(part, place.z, 0).astype(F32)
    for step in range(1, place.depth):
        total = total + swap_z(pick(part, place.z ^ step, 0), step).astype(F32)
    return total


def scatter_halves(place, grads_a, grads_b):
    part = jnp.concatenate(
        [scatter_plane(place, grads_a, "x"), scatter_plane(place, grads_b, "y")], axis=-1
    )
    return scatter_z(place, part)


def gather_small(place, row):
    stack = ordered(place.core, row, swap_core(row), 0)
    stack = spread_z(place, stack, 0)
    stack = paired(place.y, stack, swap_y(stack), 1)
    stack = paired(place.x, stack, swap_x(stack), 0)
    return stack.reshape(-1, row.shape[1])


def scatter_small(place, rows):
    grads = rows.reshape(2, place.depth, 2, 2, rows.shape[1])
    grads = pick(grads, place.core, 3) + swap_core(pick(grads, 1 - place.core, 3))
    grads = pick(grads, place.x, 0) + swap_x(pick(grads, 1 - place.x, 0))
    grads = pick(grads, place.y, 1) + swap_y(pick(grads, 1 - place.y, 1))
    total = pick(grads, place.z, 0)
    for step in range(1, place.depth):
        total = total + swap_z(pick(grads, place.z ^ step, 0), step)
    return total


def rope(values, cosine, sine):
    return values * cosine + pltpu.roll(values, HEAD_SIZE // 2, 1) * sine


def rope_back(grads, cosine, sine):
    return grads * cosine + pltpu.roll(grads * sine, HEAD_SIZE // 2, 1)


def row_scale(values):
    return lax.rsqrt(jnp.mean(values * values, axis=-1, keepdims=True) + EPSILON)


def head(ref, index):
    return ref[:, index * HEAD_SIZE : (index + 1) * HEAD_SIZE]


def dot_t(left, right):
    return lax.dot_general(left, right, (((1,), (1,)), ((), ())), preferred_element_type=F32)


def t_dot(left, right):
    return lax.dot_general(left, right, (((0,), (0,)), ((), ())), preferred_element_type=F32)


def allowed_keys(position):
    row = lax.broadcasted_iota(jnp.int32, (MB_TOK, MB_TOK), 0)
    key = lax.broadcasted_iota(jnp.int32, (MB_TOK, MB_TOK), 1)
    allowed = (key <= row) & (key >= row - position)
    return jnp.concatenate([allowed] * QUERIES_PER_KEY, axis=0)


def attend_kernel(q_ref, kv_ref, cos_ref, sin_ref, pos_ref, qg_ref, kg_ref, out_ref):
    heads = kv_ref.shape[1] // (2 * HEAD_SIZE)
    cosine, sine = cos_ref[...], sin_ref[...]
    allowed = allowed_keys(pos_ref[...])
    for j in range(heads):
        keys = head(kv_ref, j)
        key_low = rope(keys * row_scale(keys) * kg_ref[...], cosine, sine).astype(BF16)
        value = head(kv_ref, heads + j).astype(BF16)
        queries = []
        for g in range(QUERIES_PER_KEY):
            query = head(q_ref, QUERIES_PER_KEY * j + g)
            queries.append(
                rope(query * row_scale(query) * qg_ref[...], cosine, sine).astype(BF16)
            )
        scores = dot_t(jnp.concatenate(queries, axis=0), key_low) * SCALE
        scores = jnp.where(allowed, scores, MASKED)
        expo = jnp.exp(scores - jnp.max(scores, axis=-1, keepdims=True))
        probs = (expo / jnp.sum(expo, axis=-1, keepdims=True)).astype(BF16)
        mixed = jnp.dot(probs, value, preferred_element_type=F32).astype(BF16)
        for g in range(QUERIES_PER_KEY):
            index = QUERIES_PER_KEY * j + g
            out_ref[:, index * HEAD_SIZE : (index + 1) * HEAD_SIZE] = mixed[
                g * MB_TOK : (g + 1) * MB_TOK
            ]


def attend_back_kernel(
    q_ref, kv_ref, cos_ref, sin_ref, pos_ref, qg_ref, kg_ref, datt_ref,
    dq_ref, dkv_ref, sum_q_ref, sum_k_ref,
):
    heads = kv_ref.shape[1] // (2 * HEAD_SIZE)
    cosine, sine = cos_ref[...], sin_ref[...]
    allowed = allowed_keys(pos_ref[...])

    @pl.when(pl.program_id(0) == 0)
    def _():
        sum_q_ref[...] = jnp.zeros_like(sum_q_ref)
        sum_k_ref[...] = jnp.zeros_like(sum_k_ref)

    def normed_back(grad_low, raw, scale, gain):
        grad = rope_back(grad_low, cosine, sine)
        term = jnp.sum((grad * raw * scale).reshape(-1, 8, HEAD_SIZE), axis=0)
        weighted = grad * gain
        back = scale * weighted - raw * (scale * scale * scale) * jnp.mean(
            weighted * raw, axis=-1, keepdims=True
        )
        return back, term

    for j in range(heads):
        keys = head(kv_ref, j)
        key_scale = row_scale(keys)
        key_low = rope(keys * key_scale * kg_ref[...], cosine, sine).astype(BF16)
        value = head(kv_ref, heads + j).astype(BF16)
        raws, scales, lows, datts = [], [], [], []
        for g in range(QUERIES_PER_KEY):
            query = head(q_ref, QUERIES_PER_KEY * j + g)
            scale = row_scale(query)
            raws.append(query)
            scales.append(scale)
            lows.append(rope(query * scale * qg_ref[...], cosine, sine).astype(BF16))
            datts.append(head(datt_ref, QUERIES_PER_KEY * j + g))
        low = jnp.concatenate(lows, axis=0)
        datt = jnp.concatenate(datts, axis=0)
        scores = jnp.where(allowed, dot_t(low, key_low) * SCALE, MASKED)
        expo = jnp.exp(scores - jnp.max(scores, axis=-1, keepdims=True))
        probs = expo / jnp.sum(expo, axis=-1, keepdims=True)
        dprobs = dot_t(datt, value)
        dscores = (
            probs * (dprobs - jnp.sum(probs * dprobs, axis=-1, keepdims=True))
        ).astype(BF16)
        dlow = jnp.dot(dscores, key_low, preferred_element_type=F32) * SCALE
        dkey = t_dot(dscores, low) * SCALE
        dvalue = t_dot(probs.astype(BF16), datt)
        for g in range(QUERIES_PER_KEY):
            index = QUERIES_PER_KEY * j + g
            back, term = normed_back(
                dlow[g * MB_TOK : (g + 1) * MB_TOK], raws[g], scales[g], qg_ref[...]
            )
            dq_ref[:, index * HEAD_SIZE : (index + 1) * HEAD_SIZE] = back.astype(BF16)
            sum_q_ref[...] += term
        back, term = normed_back(dkey, keys, key_scale, kg_ref[...])
        dkv_ref[:, j * HEAD_SIZE : (j + 1) * HEAD_SIZE] = back.astype(BF16)
        sum_k_ref[...] += term
        index = heads + j
        dkv_ref[:, index * HEAD_SIZE : (index + 1) * HEAD_SIZE] = dvalue.astype(BF16)


def rows_spec(width):
    return pl.BlockSpec((MB_TOK, width), lambda i: (i, 0))


def same_spec(rows, width):
    return pl.BlockSpec((rows, width), lambda i: (0, 0))


def attend(q, kv, cosine, sine, position, q_gain, k_gain):
    tokens, q_width = q.shape
    kv_width = kv.shape[1]
    return pl.pallas_call(
        attend_kernel,
        grid=(tokens // MB_TOK,),
        in_specs=[rows_spec(q_width), rows_spec(kv_width)]
        + [rows_spec(HEAD_SIZE)] * 3
        + [same_spec(1, HEAD_SIZE)] * 2,
        out_specs=rows_spec(q_width),
        out_shape=jax.ShapeDtypeStruct((tokens, q_width), BF16),
        name="attend",
    )(q, kv, cosine, sine, position, q_gain, k_gain)


def attend_back(q, kv, cosine, sine, position, q_gain, k_gain, datt):
    tokens, q_width = q.shape
    kv_width = kv.shape[1]
    return pl.pallas_call(
        attend_back_kernel,
        grid=(tokens // MB_TOK,),
        in_specs=[rows_spec(q_width), rows_spec(kv_width)]
        + [rows_spec(HEAD_SIZE)] * 3
        + [same_spec(1, HEAD_SIZE)] * 2
        + [rows_spec(q_width)],
        out_specs=[
            rows_spec(q_width),
            rows_spec(kv_width),
            same_spec(8, HEAD_SIZE),
            same_spec(8, HEAD_SIZE),
        ],
        out_shape=[
            jax.ShapeDtypeStruct((tokens, q_width), BF16),
            jax.ShapeDtypeStruct((tokens, kv_width), BF16),
            jax.ShapeDtypeStruct((8, HEAD_SIZE), F32),
            jax.ShapeDtypeStruct((8, HEAD_SIZE), F32),
        ],
        name="attend_back",
    )(q, kv, cosine, sine, position, q_gain, k_gain, datt)


def rope_tables(position):
    half_width = HEAD_SIZE // 2
    frequency = ROPE_BASE ** (-2.0 * jnp.arange(half_width, dtype=F32) / HEAD_SIZE)
    angles = position[:, None] * frequency[None, :]
    cosine, sine = jnp.cos(angles), jnp.sin(angles)
    return (
        jnp.concatenate([cosine, cosine], axis=-1),
        jnp.concatenate([-sine, sine], axis=-1),
    )


def on_device(
    tokens_in,
    grad_out,
    seq_lengths,
    seq_deal,
    norm_attn,
    query_key_value_weight,
    query_norm_gain,
    k_gain,
    output_weight,
    norm_mlp,
    w_gate_up,
    w_down,
):
    place = Place()
    core = place.core
    tok_dev, width = tokens_in.shape
    query_width = QUERY_HEADS * HEAD_SIZE
    kv_width = KEY_VALUE_HEADS * HEAD_SIZE
    q_half, kv_half, out_half = query_width // 2, kv_width // 2, width // 2
    ff_block = w_down.shape[0]
    ff_half = ff_block * place.chips

    rows = query_key_value_weight.shape[0]

    def qkv_half(side):
        return jnp.concatenate(
            [
                lax.dynamic_slice_in_dim(query_key_value_weight, side * q_half, q_half, 1),
                lax.dynamic_slice_in_dim(
                    query_key_value_weight, query_width + side * kv_half, kv_half, 1
                ),
                lax.dynamic_slice_in_dim(
                    query_key_value_weight, query_width + kv_width + side * kv_half, kv_half, 1
                ),
            ],
            axis=1,
        )

    qkv_piece = ordered(core, qkv_half(core), swap_core(qkv_half(1 - core)), 0)
    out_piece = ordered(
        core,
        lax.dynamic_slice_in_dim(output_weight, core * out_half, out_half, 1),
        swap_core(lax.dynamic_slice_in_dim(output_weight, (1 - core) * out_half, out_half, 1)),
        0,
    )
    gate_split = w_gate_up.reshape(rows, 2, place.chips, 2, ff_block)
    gate_split = gate_split.transpose(3, 0, 1, 2, 4).reshape(2, rows, 2 * ff_half)
    gate_piece = ordered(core, pick(gate_split, core, 0), swap_core(pick(gate_split, 1 - core, 0)), 0)

    gain_rows, head_rows = norm_attn.shape[0], query_norm_gain.shape[0]
    small = jnp.concatenate([norm_attn, norm_mlp, query_norm_gain, k_gain])
    small_count = small.shape[0]
    small = jnp.pad(small, (0, -small_count % 128))[None, :]

    def own(values):
        return lax.dynamic_slice_in_dim(values, core * tok_dev, tok_dev, 0)

    def peer(values):
        return lax.dynamic_slice_in_dim(values, (1 - core) * tok_dev, tok_dev, 0)

    first_row = place.x * tok_dev
    own_rows = first_row + jnp.arange(tok_dev, dtype=jnp.int32)
    source, own_position = deal_rows(seq_lengths[0], seq_deal[0], own_rows)
    peer_tokens = swap_x(tokens_in)
    x_own = take_rows(tokens_in, peer_tokens, source, first_row).astype(BF16)
    x_low = ordered(core, x_own, swap_core(x_own), 0)
    own_position = own_position.astype(F32)
    position = ordered(core, own_position, swap_core(own_position), 0)
    grads_low = ordered(core, grad_out, swap_core(grad_out), 0)

    gains = gather_small(place, small)
    gain_one = gains[:, :gain_rows].reshape(1, width).astype(F32)
    gain_two = gains[:, gain_rows : 2 * gain_rows].reshape(1, width).astype(F32)
    gain_q = gains[:, 2 * gain_rows : 2 * gain_rows + head_rows].reshape(1, HEAD_SIZE).astype(F32)
    gain_k = gains[:, 2 * gain_rows + head_rows : small_count].reshape(1, HEAD_SIZE).astype(F32)

    w_q, w_kv = gather_halves(place, qkv_piece)
    w_out_a, w_out_b = gather_halves(place, out_piece)
    w_gate, w_up = gather_halves(place, gate_piece)
    w_low = gather_late_z(place, w_down)
    w_out = jnp.concatenate([w_out_a, w_out_b], axis=1)

    cosine, sine = rope_tables(position)
    position_wide = jnp.broadcast_to(position.astype(jnp.int32)[:, None], (2 * tok_dev, MB_TOK))

    x = x_low.astype(F32)
    scale_one = row_scale(x)
    normed_one = (x * scale_one * gain_one).astype(BF16)
    q = jnp.dot(normed_one, w_q, preferred_element_type=F32)
    kv = jnp.dot(normed_one, w_kv, preferred_element_type=F32)
    att = attend(q, kv, cosine, sine, position_wide, gain_q, gain_k)
    att_peer = swap_core(att)
    w_out_own = lax.dynamic_slice_in_dim(w_out, core * q_half, q_half, 0)
    w_out_peer = lax.dynamic_slice_in_dim(w_out, (1 - core) * q_half, q_half, 0)
    delta = (
        jnp.dot(att, w_out_own, preferred_element_type=F32)
        + jnp.dot(att_peer, w_out_peer, preferred_element_type=F32)
    ).astype(BF16)
    residual = x + ordered(core, delta, swap_core(delta), 1).astype(F32)
    scale_two = row_scale(residual)
    normed_two = (residual * scale_two * gain_two).astype(BF16)
    gate = jnp.dot(normed_two, w_gate, preferred_element_type=F32)
    up = jnp.dot(normed_two, w_up, preferred_element_type=F32)
    sigmoid = jax.nn.sigmoid(gate)
    activated = (gate * sigmoid * up).astype(BF16)
    down = jnp.dot(activated, w_low, preferred_element_type=F32)
    y_out = (
        own(residual) + own(down) + swap_core(peer(down).astype(BF16)).astype(F32)
    ).astype(BF16)

    term_down = t_dot(activated, grads_low).astype(BF16)
    out_down = scatter_late_xy(place, term_down)
    grad_act = dot_t(grads_low, w_low)
    grad_gate = (grad_act * up * (sigmoid * (1.0 + gate * (1.0 - sigmoid)))).astype(BF16)
    grad_up = (grad_act * (gate * sigmoid)).astype(BF16)
    term_gate = t_dot(normed_two, grad_gate).astype(BF16)
    term_up = t_dot(normed_two, grad_up).astype(BF16)
    out_gate = scatter_halves(place, term_gate, term_up)
    part_two = dot_t(grad_gate, w_gate) + dot_t(grad_up, w_up)
    grad_normed_two = part_two + swap_core(part_two.astype(BF16)).astype(F32)
    term_norm_two = jnp.sum(own(grad_normed_two * residual * scale_two), axis=0)
    grad_residual = grads_low.astype(F32) + norm_back(
        grad_normed_two, residual, scale_two, gain_two
    )
    branch = grad_residual.astype(BF16)
    branch_own = lax.dynamic_slice_in_dim(branch, core * out_half, out_half, 1)
    datt = (
        dot_t(branch_own, w_out_own)
        + swap_core(dot_t(branch_own, w_out_peer).astype(BF16)).astype(F32)
    ).astype(BF16)
    term_out_own = t_dot(att, branch_own).astype(BF16)
    term_out_peer = t_dot(att_peer, branch_own).astype(BF16)
    term_out = ordered(core, term_out_own, term_out_peer, 0)
    out_quarter = out_half // 2
    out_out = scatter_halves(place, term_out[:, :out_quarter], term_out[:, out_quarter:])
    dq, dkv, sum_q, sum_k = attend_back(
        q, kv, cosine, sine, position_wide, gain_q, gain_k, datt
    )
    term_q = t_dot(normed_one, dq).astype(BF16)
    term_kv = t_dot(normed_one, dkv).astype(BF16)
    out_qkv = scatter_halves(place, term_q, term_kv)
    part_one = dot_t(dq, w_q) + dot_t(dkv, w_kv)
    grad_normed_one = own(part_one) + swap_core(peer(part_one).astype(BF16)).astype(F32)
    x_first, scale_first = own(x), own(scale_one)
    term_norm_one = jnp.sum(grad_normed_one * x_first * scale_first, axis=0)
    grad_dealt = (
        own(grad_residual) + norm_back(grad_normed_one, x_first, scale_first, gain_one)
    ).astype(BF16)
    target = back_rows(seq_lengths[0], seq_deal[0], own_rows)
    grad_in = take_rows(grad_dealt, swap_x(grad_dealt), target, first_row)

    def unsplit(chip_rows, device_rows):
        chip_rows = chip_rows.reshape(2, device_rows, chip_rows.shape[1])
        return paired(core, pick(chip_rows, core, 0), swap_core(pick(chip_rows, 1 - core, 0)), 1)

    both = unsplit(out_qkv, rows)
    grad_qkv = jnp.concatenate(
        [
            both[:, :, :q_half].reshape(rows, query_width),
            both[:, :, q_half : q_half + kv_half].reshape(rows, kv_width),
            both[:, :, q_half + kv_half :].reshape(rows, kv_width),
        ],
        axis=1,
    )
    grad_out_proj = unsplit(out_out, output_weight.shape[0]).reshape(output_weight.shape)
    both = unsplit(out_gate, rows)
    grad_gate_up = (
        both.reshape(rows, 2, 2, place.chips, ff_block)
        .transpose(0, 2, 3, 1, 4)
        .reshape(rows, w_gate_up.shape[1])
    )

    devices = 2 * place.chips
    sums = jnp.concatenate(
        [
            term_norm_one.reshape(devices, gain_rows),
            term_norm_two.reshape(devices, gain_rows),
            jnp.sum(sum_q, axis=0).reshape(devices, head_rows),
            jnp.sum(sum_k, axis=0).reshape(devices, head_rows),
        ],
        axis=1,
    )
    sums = jnp.pad(sums, ((0, 0), (0, -small_count % 128)))
    owned = scatter_small(place, sums)
    return (
        y_out,
        grad_in,
        owned[:gain_rows],
        grad_qkv,
        owned[2 * gain_rows : 2 * gain_rows + head_rows],
        owned[2 * gain_rows + head_rows : small_count],
        grad_out_proj,
        owned[gain_rows : 2 * gain_rows],
        grad_gate_up,
        out_down,
    )


def norm_back(grad_norm, inputs, scale, gain):
    weighted = grad_norm * gain
    return scale * weighted - inputs * (scale * scale * scale) * jnp.mean(
        weighted * inputs, axis=-1, keepdims=True
    )


def scatter_late_xy(place, grads):
    depth = place.depth
    rows, cols = grads.shape[0] // (4 * depth), grads.shape[1]
    half = cols // 2
    grads = grads.reshape(2, depth, 2, rows, cols)
    total = pick(grads, place.z, 1).astype(F32)
    for step in range(1, depth):
        total = total + swap_z(pick(grads, place.z ^ step, 1), step).astype(F32)
    total = total.astype(BF16)
    first, second = total[..., :half], total[..., half:]
    first = add(pick(first, place.y, 1), swap_y(pick(first, 1 - place.y, 1)))
    first = pick(first, place.x, 0).astype(F32) + swap_x(pick(first, 1 - place.x, 0)).astype(F32)
    second = add(pick(second, place.x, 0), swap_x(pick(second, 1 - place.x, 0)))
    second = pick(second, place.y, 0).astype(F32) + swap_y(pick(second, 1 - place.y, 0)).astype(
        F32
    )
    return jnp.concatenate([first, second], axis=1)


def solution(mesh):
    rows = P(("grp", "dp"), None)
    line = P(("grp", "dp"))
    return jax.shard_map(
        on_device,
        mesh=mesh,
        in_specs=(rows, rows, P("dp", None), P("dp", None), line, rows, line, line, rows, line, rows, rows),
        out_specs=(rows, rows, line, rows, line, line, rows, line, rows, rows),
        check_vma=False,
    )
```

time: 1130 us -> 603 us (0.53)
  waiting for transfers between devices: 779 us -> 312 us
  starting transfers between devices: 3.95 us -> 103 us
  blocking collectives: 96.1 us -> 0 us
  matrix products: 130 us -> 53.6 us
  Pallas kernels: 0 us -> 23.7 us
  other arithmetic: 39.4 us -> 60.4 us
  local copies, waits for them, and re-layouts: 53.4 us -> 37.5 us
  between operations: 16.3 us -> 2.69 us
    reduce_scatter x4 -> x0, waiting for transfers between devices: 573 us -> none  [the longest x1 254 us: on_device(): lax.psum_scatter(terms[2], ('grp', 'dp'), scatter_dimension=0, tiled=True)]
    ppermute x2 -> x85, waiting for transfers between devices: 0.01 us -> 312 us  [swap(): return lax.ppermute(values, axis, [(i, i ^ mask) for i in range(size)])]
    all_gather x4 -> x0, waiting for transfers between devices: 203 us -> none  [the longest x1 89.5 us: fetch_feedforward(): lax.all_gather(w_gate_up, ('grp', 'dp'), axis=0, tiled=True)]
    ppermute x2 -> x85, starting transfers between devices: 3.23 us -> 103 us  [swap(): return lax.ppermute(values, axis, [(i, i ^ mask) for i in range(size)])]
    unnamed x2 -> x0, blocking collectives: 96.1 us -> none
    dot_general x32 -> x25, matrix products: 130 us -> 53.6 us  [the longest x7 18 us: dot_t(): lax.dot_general(left, right, (((1,), (1,)), ((), ())), preferred_element_...]
    pallas_call x0 -> x2, Pallas kernels: none -> 23.7 us  [the longest x1 15.1 us: attend_back(): pl.pallas_call(attend_back_kernel, grid=(tokens // MB_TOK,), in_specs=[ro...]
    unnamed x296 -> x112, local copies, waits for them, and re-layouts: 22.4 us -> 4.11 us
  transfers between devices with their start and end apart: 10 -> 85, of which waited for: 7 -> 30; matrix products, arithmetic and copies ran while one was open for 15% -> 22% of each run, Pallas kernels for 0% -> 4%
where the time goes in v1:
time: 603 us; the launch traced here: 593 us
  waiting for transfers between devices  312 us (52%)
  starting transfers between devices  103 us (17%)
  other arithmetic  60.4 us (10%)
  matrix products  53.6 us (9%)
  local copies, waits for them, and re-layouts  37.5 us (6%)
  Pallas kernels  23.7 us (4%)
    ppermute x85, waiting for transfers between devices, swap(): return lax.ppermute(values, axis, [(i, i ^ mask) for i in range(size)])  312 us
    ppermute x85, starting transfers between devices, swap(): return lax.ppermute(values, axis, [(i, i ^ mask) for i in range(size)])  103 us
    dot_general x7, matrix products, dot_t(): lax.dot_general(left, right, (((1,), (1,)), ((), ())), preferred_element_...  18 us
    select_n x54, other arithmetic, ordered(): jnp.where(bit == 0, jnp.concatenate([own, peer], axis=axis), jnp.concaten...  16.8 us
    dot_general x7, matrix products, t_dot(): lax.dot_general(left, right, (((0,), (0,)), ((), ())), preferred_element_...  15.5 us
    pallas_call x1, Pallas kernels, attend_back(): pl.pallas_call(attend_back_kernel, grid=(tokens // MB_TOK,), in_specs=[ro...  15.1 us
  transfers between devices with their start and end apart: 85, of which 30 were waited for; matrix products, arithmetic and copies ran while one was open for 22% of the time, Pallas kernels for 4%

profile of v1, /device:TPU:1, one launch (start us, length us, event | category | flops | bytes accessed | tf_op | source)
XLA Modules:
  0.0 593.4 jit_solution(7659784960572012)
XLA Ops:
  17.0 3.4 collective-permute-start.5
  34.5 5.3 collective-permute-start.27
  48.1 4.8 collective-permute-done.19
  63.8 11.7 %collective-permute-done.10 = bf16[64,2048]{1,0:T(8,128)(2,1)S(1)} collective-permute-done((bf16[64,2048]{1,0:T(8,128)(2,1)S(1)}, bf16[64,2048]{1,0:T(8,128)(2,1)S(1)}, u32[]{:S(2)}, u32[]{:S(2)}) %collective-permute-start.10) | collective-permute-done | bytes 262176 | tf_op jit(solution)/shard_map/ppermute | solution.py:74
  86.5 55.1 %collective-permute-done.29 = bf16[64,3072]{1,0:T(8,128)(2,1)S(1)} collective-permute-done((bf16[64,3072]{1,0:T(8,128)(2,1)S(1)}, bf16[64,3072]{1,0:T(8,128)(2,1)S(1)}, u32[]{:S(2)}, u32[]{:S(2)}) %collective-permute-start.29) | collective-permute-done | bytes 393248 | tf_op jit(solution)/shard_map/ppermute | solution.py:74
  149.7 11.9 %collective-permute-start.1 = (bf16[256,1024]{1,0:T(8,128)(2,1)S(1)}, bf16[256,1024]{1,0:T(8,128)(2,1)S(1)}, u32[]{:S(2)}, u32[]{:S(2)}) collective-permute-start(bf16[256,1024]{1,0:T(8,128)(2,1)S(1)} %fusion.11), channel_id=1, source_target_pairs={{0,1},{1,0},{2,3},{3,2},{4,5},{5,4},{6,7},{7,6},{8,9},{9,8},{10,11... | collective-permute-start | bytes 1572872 | tf_op jit(solution)/shard_map/ppermute | solution.py:74
  168.1 26.9 %collective-permute-done.39 = bf16[2,2,96,1024]{3,2,1,0:T(8,128)(2,1)S(1)} collective-permute-done((bf16[2,2,96,1024]{3,2,1,0:T(8,128)(2,1)S(1)}, bf16[2,2,96,1024]{3,2,1,0:T(8,128)(2,1)S(1)}, u32[]{:S(2)}, u32[]{:S(2)}) %collective-permute-start.39) | collective-permute-done | bytes 786464 | tf_op jit(solution)/shard_map/ppermute | solution.py:74
  205.0 14.3 %collective-permute-done.13 = bf16[4,2,64,1024]{3,2,1,0:T(8,128)(2,1)S(1)} collective-permute-done((bf16[4,2,64,1024]{3,2,1,0:T(8,128)(2,1)S(1)}, bf16[4,2,64,1024]{3,2,1,0:T(8,128)(2,1)S(1)}, u32[]{:S(2)}, u32[]{:S(2)}) %collective-permute-start.13) | collective-permute-done | bytes 1048608 | tf_op jit(solution)/shard_map/ppermute | solution.py:74
  227.1 8.6 %attend.1 = bf16[512,1024]{1,0:T(8,128)(2,1)} custom-call(f32[512,1024]{1,0:T(8,128)} %fusion.91.q_ref, f32[512,1024]{1,0:T(8,128)} %fusion.90.kv_ref, f32[512,128]{1,0:T(8,128)} %get-tuple-element.128.cos_ref, f32[512,128]{1,0:T(8,128)} %get-tuple-element.129.sin_ref, s32[512,128]{1,0:T(8,128)} %broadcast_in_dim.193.pos_ref, f32[1,128]{1,0:T(1,128)} %reshape.1433.qg_ref, ...), custom_call_target="tpu_custom_call" | custom-call | tf_op jit(solution)/shard_map/attend/pallas_call | solution.py:347
  237.2 4.5 fusion.89
  246.6 10.1 %collective-permute-done.34 = bf16[2,4,64,1536]{3,2,1,0:T(8,128)(2,1)} collective-permute-done((bf16[2,4,64,1536]{3,2,1,0:T(8,128)(2,1)}, bf16[2,4,64,1536]{3,2,1,0:T(8,128)(2,1)}, u32[]{:S(2)}, u32[]{:S(2)}) %collective-permute-start.34) | collective-permute-done | bytes 1572896 | tf_op jit(solution)/shard_map/ppermute | solution.py:74
  289.1 11.5 %collective-permute-done.80 = bf16[2,2,96,1024]{3,2,1,0:T(8,128)(2,1)S(1)} collective-permute-done((bf16[2,2,96,1024]{3,2,1,0:T(8,128)(2,1)S(1)}, bf16[2,2,96,1024]{3,2,1,0:T(8,128)(2,1)S(1)}, u32[]{:S(2)}, u32[]{:S(2)}) %collective-permute-start.80) | collective-permute-done | bytes 786464 | tf_op jit(solution)/shard_map/ppermute | solution.py:74
  300.8 47.4 %collective-permute-done.79 = bf16[2,2,96,1024]{3,2,1,0:T(8,128)(2,1)S(1)} collective-permute-done((bf16[2,2,96,1024]{3,2,1,0:T(8,128)(2,1)S(1)}, bf16[2,2,96,1024]{3,2,1,0:T(8,128)(2,1)S(1)}, u32[]{:S(2)}, u32[]{:S(2)}) %collective-permute-start.79) | collective-permute-done | bytes 786464 | tf_op jit(solution)/shard_map/ppermute | solution.py:74
  354.9 34.0 %collective-permute-done.81 = bf16[2,96,512]{2,1,0:T(8,128)(2,1)S(1)} collective-permute-done((bf16[2,96,512]{2,1,0:T(8,128)(2,1)S(1)}, bf16[2,96,512]{2,1,0:T(8,128)(2,1)S(1)}, u32[]{:S(2)}, u32[]{:S(2)}) %collective-permute-start.81) | collective-permute-done | bytes 196640 | tf_op jit(solution)/shard_map/ppermute | solution.py:74
  398.1 3.4 collective-permute-start.45
  411.0 9.9 %collective-permute-done.62 = bf16[4,2,128,256]{3,2,0,1:T(8,128)(2,1)S(1)} collective-permute-done((bf16[4,2,128,256]{3,2,0,1:T(8,128)(2,1)S(1)}, bf16[4,2,128,256]{3,2,0,1:T(8,128)(2,1)S(1)}, u32[]{:S(2)}, u32[]{:S(2)}) %collective-permute-start.62) | collective-permute-done | bytes 524320 | tf_op jit(solution)/shard_map/ppermute | solution.py:74
  436.0 6.3 %collective-permute-done.67 = bf16[128,512]{1,0:T(8,128)(2,1)S(1)} collective-permute-done((bf16[128,512]{1,0:T(8,128)(2,1)S(1)}, bf16[128,512]{1,0:T(8,128)(2,1)S(1)}, u32[]{:S(2)}, u32[]{:S(2)}) %collective-permute-start.67) | collective-permute-done | bytes 131104 | tf_op jit(solution)/shard_map/ppermute | solution.py:74
  447.1 15.1 %attend_back.1 = (bf16[512,1024]{1,0:T(8,128)(2,1)}, bf16[512,1024]{1,0:T(8,128)(2,1)}, f32[8,128]{1,0:T(8,128)}, f32[8,128]{1,0:T(8,128)}) custom-call(f32[512,1024]{1,0:T(8,128)} %fusion.91.q_ref, f32[512,1024]{1,0:T(8,128)} %fusion.90.kv_ref, f32[512,128]{1,0:T(8,128)} %get-tuple-element.128.cos_ref, f32[512,128]{1,0:T(8,128)} %get-tuple-element.129.sin_ref, ...), custom_call_target="tpu_custom_call" | custom-call | tf_op jit(solution)/shard_map/attend_back/pallas_call | solution.py:362
  492.0 10.9 %collective-permute-done.49 = f32[4,2,128]{2,1,0:T(2,128)S(1)} collective-permute-done((f32[4,2,128]{2,1,0:T(2,128)S(1)}, f32[4,2,128]{2,1,0:T(2,128)S(1)}, u32[]{:S(2)}, u32[]{:S(2)}) %collective-permute-start.49) | collective-permute-done | bytes 4128 | tf_op jit(solution)/shard_map/ppermute | solution.py:74
  516.4 6.0 %collective-permute-done.76 = bf16[64,3072]{1,0:T(8,128)(2,1)S(1)} collective-permute-done((bf16[64,3072]{1,0:T(8,128)(2,1)S(1)}, bf16[64,3072]{1,0:T(8,128)(2,1)S(1)}, u32[]{:S(2)}, u32[]{:S(2)}) %collective-permute-start.76) | collective-permute-done | bytes 393248 | tf_op jit(solution)/shard_map/ppermute | solution.py:74
  523.6 22.5 %collective-permute-done.75 = bf16[64,3072]{1,0:T(8,128)(2,1)S(1)} collective-permute-done((bf16[64,3072]{1,0:T(8,128)(2,1)S(1)}, bf16[64,3072]{1,0:T(8,128)(2,1)S(1)}, u32[]{:S(2)}, u32[]{:S(2)}) %collective-permute-start.75) | collective-permute-done | bytes 393248 | tf_op jit(solution)/shard_map/ppermute | solution.py:74
  555.2 3.9 collective-permute-done.55
  573.6 10.3 %collective-permute-done.59 = bf16[64,2048]{1,0:T(8,128)(2,1)} collective-permute-done((bf16[64,2048]{1,0:T(8,128)(2,1)}, bf16[64,2048]{1,0:T(8,128)(2,1)}, u32[]{:S(2)}, u32[]{:S(2)}) %collective-permute-start.59) | collective-permute-done | bytes 262176 | tf_op jit(solution)/shard_map/ppermute | solution.py:74
  585.1 3.6 collective-permute-start.61
  (489 shorter events, 249.2 us)
Async XLA Ops:
  3.2 37.9 %collective-permute-start.8 = (bf16[32,2048]{1,0:T(8,128)(2,1)}, bf16[32,2048]{1,0:T(8,128)(2,1)S(1)}, u32[]{:S(2)}, u32[]{:S(2)}) collective-permute-start(bf16[32,2048]{1,0:T(8,128)(2,1)} %pad_maximum_fusion.11), channel_id=1, source_target_pairs={{0,1},{1,0},{2,3},{3,2},{4,5},{5,4},{6,7},{7,6},{8,9},{9,8},{10,11... | collective-permute-start | bytes 393224 | tf_op jit(solution)/shard_map/ppermute | solution.py:74
  4.5 78.0 %collective-permute-start = (bf16[256,1024]{1,0:T(8,128)(2,1)}, bf16[256,1024]{1,0:T(8,128)(2,1)S(1)}, u32[]{:S(2)}, u32[]{:S(2)}) collective-permute-start(bf16[256,1024]{1,0:T(8,128)(2,1)} %param.12), channel_id=1, source_target_pairs={{0,16},{16,0},{1,17},{17,1},{2,18},{18,2},{3,19},{19,3},{4,20},{20... | collective-permute-start | bytes 1572872 | tf_op jit(solution)/shard_map/ppermute | solution.py:74
  77.7 64.0 %collective-permute-start.29 = (bf16[64,3072]{1,0:T(8,128)(2,1)S(1)}, bf16[64,3072]{1,0:T(8,128)(2,1)S(1)}, u32[]{:S(2)}, u32[]{:S(2)}) collective-permute-start(bf16[64,3072]{1,0:T(8,128)(2,1)S(1)} %maximum_select_fusion.32), channel_id=1, source_target_pairs={{0,8},{1,9},{2,10},{3,11},{4,12},{5,13},{6,14},{7,15},{8,0},{9,1},... | collective-permute-start | bytes 1179656 | tf_op jit(solution)/shard_map/ppermute | solution.py:74
  78.4 64.7 %collective-permute-start.28 = (bf16[64,3072]{1,0:T(8,128)(2,1)S(1)}, bf16[64,3072]{1,0:T(8,128)(2,1)S(1)}, u32[]{:S(2)}, u32[]{:S(2)}) collective-permute-start(bf16[64,3072]{1,0:T(8,128)(2,1)S(1)} %maximum_select_fusion.32), channel_id=1, source_target_pairs={{0,4},{1,5},{2,6},{3,7},{4,0},{5,1},{6,2},{7,3},{8,12},{9,13},{10,... | collective-permute-start | bytes 1179656 | tf_op jit(solution)/shard_map/ppermute | solution.py:74
  80.0 117.4 %collective-permute-start.41 = (bf16[2,2,96,1024]{3,2,1,0:T(8,128)(2,1)S(1)}, bf16[2,2,96,1024]{3,2,1,0:T(8,128)(2,1)S(1)}, u32[]{:S(2)}, u32[]{:S(2)}) collective-permute-start(bf16[2,2,96,1024]{3,2,1,0:T(8,128)(2,1)S(1)} %get-tuple-element.72), channel_id=1, source_target_pairs={{0,12},{1,13},{2,14},{3,15},{4,8},{5,9},{6,10},{7,11},{8,4},{9,5},... | collective-permute-start | bytes 2359304 | tf_op jit(solution)/shard_map/ppermute | solution.py:74
  82.5 115.7 %collective-permute-start.40 = (bf16[2,2,96,1024]{3,2,1,0:T(8,128)(2,1)S(1)}, bf16[2,2,96,1024]{3,2,1,0:T(8,128)(2,1)S(1)}, u32[]{:S(2)}, u32[]{:S(2)}) collective-permute-start(bf16[2,2,96,1024]{3,2,1,0:T(8,128)(2,1)S(1)} %get-tuple-element.72), channel_id=1, source_target_pairs={{0,8},{1,9},{2,10},{3,11},{4,12},{5,13},{6,14},{7,15},{8,0},{9,1},... | collective-permute-start | bytes 2359304 | tf_op jit(solution)/shard_map/ppermute | solution.py:74
  85.9 59.5 %collective-permute-start.12 = (bf16[4,64,1024]{2,1,0:T(8,128)(2,1)S(1)}, bf16[4,64,1024]{2,1,0:T(8,128)(2,1)S(1)}, u32[]{:S(2)}, u32[]{:S(2)}) collective-permute-start(bf16[4,64,1024]{2,1,0:T(8,128)(2,1)S(1)} %get-tuple-element.64), channel_id=1, source_target_pairs={{0,2},{1,3},{2,0},{3,1},{4,6},{5,7},{6,4},{7,5},{8,10},{9,11},{10,... | collective-permute-start | bytes 1572872 | tf_op jit(solution)/shard_map/ppermute | solution.py:74
  163.4 37.6 %collective-permute-start.33 = (bf16[4,64,1536]{2,1,0:T(8,128)(2,1)S(1)}, bf16[4,64,1536]{2,1,0:T(8,128)(2,1)S(1)}, u32[]{:S(2)}, u32[]{:S(2)}) collective-permute-start(bf16[4,64,1536]{2,1,0:T(8,128)(2,1)S(1)} %get-tuple-element.52), channel_id=1, source_target_pairs={{0,16},{16,0},{1,17},{17,1},{2,18},{18,2},{3,19},{19,3},{4,20},{20... | collective-permute-start | bytes 2359304 | tf_op jit(solution)/shard_map/ppermute | solution.py:74
  197.4 39.9 %collective-permute-start.43 = (bf16[256,1024]{1,0:T(8,128)(2,1)}, bf16[256,1024]{1,0:T(8,128)(2,1)}, u32[]{:S(2)}, u32[]{:S(2)}) collective-permute-start(bf16[256,1024]{1,0:T(8,128)(2,1)} %param.13), channel_id=1, source_target_pairs={{0,1},{1,0},{2,3},{3,2},{4,5},{5,4},{6,7},{7,6},{8,9},{9,8},{10,11... | collective-permute-start | bytes 1572872 | tf_op jit(solution)/shard_map/ppermute | solution.py:74
  202.5 54.2 %collective-permute-start.34 = (bf16[2,4,64,1536]{3,2,1,0:T(8,128)(2,1)}, bf16[2,4,64,1536]{3,2,1,0:T(8,128)(2,1)}, u32[]{:S(2)}, u32[]{:S(2)}) collective-permute-start(bf16[2,4,64,1536]{3,2,1,0:T(8,128)(2,1)} %maximum_select_fusion.10), channel_id=1, source_target_pairs={{0,2},{1,3},{2,0},{3,1},{4,6},{5,7},{6,4},{7,5},{8,10},{9,11},{10,... | collective-permute-start | bytes 4718600 | tf_op jit(solution)/shard_map/ppermute | solution.py:74
  204.8 54.6 %collective-permute-start.32 = (bf16[4,2,64,1536]{3,2,0,1:T(8,128)(2,1)}, bf16[4,2,64,1536]{3,2,0,1:T(8,128)(2,1)}, u32[]{:S(2)}, u32[]{:S(2)}) collective-permute-start(bf16[4,2,64,1536]{3,2,0,1:T(8,128)(2,1)} %maximum_select_fusion.8), channel_id=1, source_target_pairs={{0,16},{16,0},{1,17},{17,1},{2,18},{18,2},{3,19},{19,3},{4,20},{20... | collective-permute-start | bytes 4718600 | tf_op jit(solution)/shard_map/ppermute | solution.py:74
  273.8 116.4 %collective-permute-start.44 = (bf16[512,1024]{1,0:T(8,128)(2,1)S(1)}, bf16[512,1024]{1,0:T(8,128)(2,1)S(1)}, u32[]{:S(2)}, u32[]{:S(2)}) collective-permute-start(bf16[512,1024]{1,0:T(8,128)(2,1)S(1)} %get-tuple-element.126), channel_id=1, source_target_pairs={{0,1},{1,0},{2,3},{3,2},{4,5},{5,4},{6,7},{7,6},{8,9},{9,8},{10,11... | collective-permute-start | bytes 3145736 | tf_op jit(solution)/shard_map/ppermute | solution.py:74
  282.5 65.7 %collective-permute-start.79 = (bf16[2,2,96,1024]{3,2,1,0:T(8,128)(2,1)S(1)}, bf16[2,2,96,1024]{3,2,1,0:T(8,128)(2,1)S(1)}, u32[]{:S(2)}, u32[]{:S(2)}) collective-permute-start(bf16[2,2,96,1024]{3,2,1,0:T(8,128)(2,1)S(1)} %get-tuple-element.38), channel_id=1, source_target_pairs={{0,8},{1,9},{2,10},{3,11},{4,12},{5,13},{6,14},{7,15},{8,0},{9,1},... | collective-permute-start | bytes 2359304 | tf_op jit(solution)/shard_map/ppermute | solution.py:74
  282.5 65.7 %collective-permute-start.78 = (bf16[2,2,96,1024]{3,2,1,0:T(8,128)(2,1)S(1)}, bf16[2,2,96,1024]{3,2,1,0:T(8,128)(2,1)S(1)}, u32[]{:S(2)}, u32[]{:S(2)}) collective-permute-start(bf16[2,2,96,1024]{3,2,1,0:T(8,128)(2,1)S(1)} %get-tuple-element.36), channel_id=1, source_target_pairs={{0,4},{1,5},{2,6},{3,7},{4,0},{5,1},{6,2},{7,3},{8,12},{9,13},{10,... | collective-permute-start | bytes 2359304 | tf_op jit(solution)/shard_map/ppermute | solution.py:74
  284.1 113.9 %collective-permute-start.42 = (bf16[256,1024]{1,0:T(8,128)(2,1)S(1)}, bf16[256,1024]{1,0:T(8,128)(2,1)S(1)}, u32[]{:S(2)}, u32[]{:S(2)}) collective-permute-start(bf16[256,1024]{1,0:T(8,128)(2,1)S(1)} %dynamic-slice_convert_fusion.2), channel_id=1, source_target_pairs={{0,1},{1,0},{2,3},{3,2},{4,5},{5,4},{6,7},{7,6},{8,9},{9,8},{10,11... | collective-permute-start | bytes 1572872 | tf_op jit(solution)/shard_map/ppermute | solution.py:74
  300.6 122.7 %collective-permute-start.70 = (bf16[4,2,64,1536]{3,2,1,0:T(8,128)(2,1)}, bf16[4,2,64,1536]{3,2,1,0:T(8,128)(2,1)}, u32[]{:S(2)}, u32[]{:S(2)}) collective-permute-start(bf16[4,2,64,1536]{3,2,1,0:T(8,128)(2,1)} %dynamic-slice_bitcast_fusion.1), channel_id=1, source_target_pairs={{0,16},{16,0},{1,17},{17,1},{2,18},{18,2},{3,19},{19,3},{4,20},{20... | collective-permute-start | bytes 4718600 | tf_op jit(solution)/shard_map/ppermute | solution.py:74
  350.5 76.6 %collective-permute-start.72 = (bf16[2,4,64,1536]{3,2,1,0:T(8,128)(2,1)}, bf16[2,4,64,1536]{3,2,1,0:T(8,128)(2,1)}, u32[]{:S(2)}, u32[]{:S(2)}) collective-permute-start(bf16[2,4,64,1536]{3,2,1,0:T(8,128)(2,1)} %dynamic-slice_bitcast_fusion), channel_id=1, source_target_pairs={{0,2},{1,3},{2,0},{3,1},{4,6},{5,7},{6,4},{7,5},{8,10},{9,11},{10,... | collective-permute-start | bytes 4718600 | tf_op jit(solution)/shard_map/ppermute | solution.py:74
  398.1 45.7 %collective-permute-start.45 = (bf16[512,1024]{1,0:T(8,128)(2,1)}, bf16[512,1024]{1,0:T(8,128)(2,1)}, u32[]{:S(2)}, u32[]{:S(2)}) collective-permute-start(bf16[512,1024]{1,0:T(8,128)(2,1)} %convolution_convert_fusion.7), channel_id=1, source_target_pairs={{0,1},{1,0},{2,3},{3,2},{4,5},{5,4},{6,7},{7,6},{8,9},{9,8},{10,11... | collective-permute-start | bytes 3145736 | tf_op jit(solution)/shard_map/ppermute | solution.py:74
  426.2 57.7 %collective-permute-start.71 = (bf16[4,64,1536]{2,1,0:T(8,128)(2,1)}, bf16[4,64,1536]{2,1,0:T(8,128)(2,1)}, u32[]{:S(2)}, u32[]{:S(2)}) collective-permute-start(bf16[4,64,1536]{2,1,0:T(8,128)(2,1)} %dynamic-slice_bitcast_fusion.8), channel_id=1, source_target_pairs={{0,2},{1,3},{2,0},{3,1},{4,6},{5,7},{6,4},{7,5},{8,10},{9,11},{10,... | collective-permute-start | bytes 2359304 | tf_op jit(solution)/shard_map/ppermute | solution.py:74
  435.0 50.4 %collective-permute-start.73 = (bf16[4,64,1536]{2,1,0:T(8,128)(2,1)}, bf16[4,64,1536]{2,1,0:T(8,128)(2,1)}, u32[]{:S(2)}, u32[]{:S(2)}) collective-permute-start(bf16[4,64,1536]{2,1,0:T(8,128)(2,1)} %dynamic-slice_bitcast_fusion.7), channel_id=1, source_target_pairs={{0,16},{16,0},{1,17},{17,1},{2,18},{18,2},{3,19},{19,3},{4,20},{20... | collective-permute-start | bytes 2359304 | tf_op jit(solution)/shard_map/ppermute | solution.py:74
  442.4 39.4 %collective-permute-start.69 = (f32[64,512]{1,0:T(8,128)S(1)}, f32[64,512]{1,0:T(8,128)S(1)}, u32[]{:S(2)}, u32[]{:S(2)}) collective-permute-start(f32[64,512]{1,0:T(8,128)S(1)} %get-tuple-element.91), channel_id=1, source_target_pairs={{0,1},{1,0},{2,3},{3,2},{4,5},{5,4},{6,7},{7,6},{8,9},{9,8},{10,11... | collective-permute-start | bytes 393224 | tf_op jit(solution)/shard_map/ppermute | solution.py:74
  478.2 68.1 %collective-permute-start.54 = (bf16[4,2,64,1024]{3,2,1,0:T(8,128)(2,1)}, bf16[4,2,64,1024]{3,2,1,0:T(8,128)(2,1)}, u32[]{:S(2)}, u32[]{:S(2)}) collective-permute-start(bf16[4,2,64,1024]{3,2,1,0:T(8,128)(2,1)} %dynamic-slice_bitcast_fusion.3), channel_id=1, source_target_pairs={{0,16},{16,0},{1,17},{17,1},{2,18},{18,2},{3,19},{19,3},{4,20},{20... | collective-permute-start | bytes 3145736 | tf_op jit(solution)/shard_map/ppermute | solution.py:74
  481.8 67.3 %collective-permute-start.56 = (bf16[2,4,64,1024]{3,2,1,0:T(8,128)(2,1)}, bf16[2,4,64,1024]{3,2,1,0:T(8,128)(2,1)}, u32[]{:S(2)}, u32[]{:S(2)}) collective-permute-start(bf16[2,4,64,1024]{3,2,1,0:T(8,128)(2,1)} %dynamic-slice_bitcast_fusion.2), channel_id=1, source_target_pairs={{0,2},{1,3},{2,0},{3,1},{4,6},{5,7},{6,4},{7,5},{8,10},{9,11},{10,... | collective-permute-start | bytes 3145736 | tf_op jit(solution)/shard_map/ppermute | solution.py:74
  522.4 66.2 %collective-permute-start.47 = (bf16[256,1024]{1,0:T(8,128)(2,1)}, bf16[256,1024]{1,0:T(8,128)(2,1)}, u32[]{:S(2)}, u32[]{:S(2)}) collective-permute-start(bf16[256,1024]{1,0:T(8,128)(2,1)} %add_convert_fusion.1), channel_id=1, source_target_pairs={{0,16},{16,0},{1,17},{17,1},{2,18},{18,2},{3,19},{19,3},{4,20},{20... | collective-permute-start | bytes 1572872 | tf_op jit(solution)/shard_map/ppermute | solution.py:74
  (115 other events, 1607.6 us)

commit v2 on v1

--- a/solution.py
+++ b/solution.py
@@ -69,36 +69,39 @@
     )
 
 
+CHIPS = ("x", "z", "y")
+DEVICES = ("x", "z", "y", "core")
+
+
 def swap(values, axis, mask):
     size = lax.axis_size(axis)
     return lax.ppermute(values, axis, [(i, i ^ mask) for i in range(size)])
 
 
 def swap_core(values):
-    return swap(values, "dp", 1)
+    return swap(values, "core", 1)
 
 
 def swap_y(values):
-    return swap(values, "dp", 2)
+    return swap(values, "y", 1)
 
 
 def swap_z(values, step):
-    return swap(values, "dp", 4 * step)
+    return swap(values, "z", step)
 
 
 def swap_x(values):
-    return swap(values, "grp", 1)
+    return swap(values, "x", 1)
 
 
 class Place:
     def __init__(self):
-        index = lax.axis_index("dp")
-        self.x = lax.axis_index("grp")
-        self.core = index % 2
-        self.y = (index // 2) % 2
-        self.z = index // 4
-        self.depth = lax.axis_size("dp") // 4
-        self.chips = lax.axis_size("dp")
+        self.x = lax.axis_index("x")
+        self.core = lax.axis_index("core")
+        self.y = lax.axis_index("y")
+        self.z = lax.axis_index("z")
+        self.depth = lax.axis_size("z")
+        self.chips = 4 * self.depth
 
 
 def ordered(bit, own, peer, axis):
@@ -153,18 +156,6 @@
         gather_late_x(place, stack[..., :half]),
         gather_late_y(place, stack[..., half:]),
     )
-
-
-def gather_late_z(place, piece):
-    half = piece.shape[1] // 2
-    first, second = piece[:, :half], piece[:, half:]
-    first = paired(place.x, first, swap_x(first), 0)
-    first = paired(place.y, first, swap_y(first), 1)
-    second = paired(place.y, second, swap_y(second), 0)
-    second = paired(place.x, second, swap_x(second), 0)
-    both = jnp.concatenate([first, second], axis=-1)
-    stack = spread_z(place, both, 1)
-    return stack.reshape(-1, stack.shape[-1])
 
 
 def add(first, second):
@@ -473,7 +464,7 @@
     w_q, w_kv = gather_halves(place, qkv_piece)
     w_out_a, w_out_b = gather_halves(place, out_piece)
     w_gate, w_up = gather_halves(place, gate_piece)
-    w_low = gather_late_z(place, w_down)
+    w_low = lax.all_gather(w_down, CHIPS, axis=0, tiled=True)
     w_out = jnp.concatenate([w_out_a, w_out_b], axis=1)
 
     cosine, sine = rope_tables(position)
@@ -505,7 +496,7 @@
     ).astype(BF16)
 
     term_down = t_dot(activated, grads_low).astype(BF16)
-    out_down = scatter_late_xy(place, term_down)
+    out_down = lax.psum_scatter(term_down, CHIPS, scatter_dimension=0, tiled=True).astype(F32)
     grad_act = dot_t(grads_low, w_low)
     grad_gate = (grad_act * up * (sigmoid * (1.0 + gate * (1.0 - sigmoid)))).astype(BF16)
     grad_up = (grad_act * (gate * sigmoid)).astype(BF16)
@@ -599,32 +590,14 @@
     )
 
 
-def scatter_late_xy(place, grads):
-    depth = place.depth
-    rows, cols = grads.shape[0] // (4 * depth), grads.shape[1]
-    half = cols // 2
-    grads = grads.reshape(2, depth, 2, rows, cols)
-    total = pick(grads, place.z, 1).astype(F32)
-    for step in range(1, depth):
-        total = total + swap_z(pick(grads, place.z ^ step, 1), step).astype(F32)
-    total = total.astype(BF16)
-    first, second = total[..., :half], total[..., half:]
-    first = add(pick(first, place.y, 1), swap_y(pick(first, 1 - place.y, 1)))
-    first = pick(first, place.x, 0).astype(F32) + swap_x(pick(first, 1 - place.x, 0)).astype(F32)
-    second = add(pick(second, place.x, 0), swap_x(pick(second, 1 - place.x, 0)))
-    second = pick(second, place.y, 0).astype(F32) + swap_y(pick(second, 1 - place.y, 0)).astype(
-        F32
-    )
-    return jnp.concatenate([first, second], axis=1)
-
-
 def solution(mesh):
-    rows = P(("grp", "dp"), None)
-    line = P(("grp", "dp"))
+    groups, size = mesh.shape["grp"], mesh.shape["dp"]
+    mesh = jax.sharding.Mesh(mesh.devices.reshape(groups, size // 4, 2, 2), DEVICES)
+    rows, line, pairs = P(DEVICES, None), P(DEVICES), P(("z", "y", "core"), None)
     return jax.shard_map(
         on_device,
         mesh=mesh,
-        in_specs=(rows, rows, P("dp", None), P("dp", None), line, rows, line, line, rows, line, rows, rows),
+        in_specs=(rows, rows, pairs, pairs, line, rows, line, line, rows, line, rows, rows),
         out_specs=(rows, rows, line, rows, line, line, rows, line, rows, rows),
         check_vma=False,
     )

time: 603 us -> 517 us (0.86)
  waiting for transfers between devices: 312 us -> 232 us
  starting transfers between devices: 103 us -> 82.2 us
  between operations: 2.69 us -> 16.2 us
    ppermute x85 -> x71, waiting for transfers between devices: 312 us -> 232 us  [swap(): return lax.ppermute(values, axis, [(i, i ^ mask) for i in range(size)])]
    ppermute x85 -> x71, starting transfers between devices: 103 us -> 82.2 us  [swap(): return lax.ppermute(values, axis, [(i, i ^ mask) for i in range(size)])]
    select_n x54 -> x45, other arithmetic: 16.8 us -> 14.1 us  [ordered(): jnp.where(bit == 0, jnp.concatenate([own, peer], axis=axis), jnp.concaten...]
    convert_element_type x14 -> x12, other arithmetic: 11.7 us -> 13.9 us  [add(): return (first.astype(F32) + second.astype(F32)).astype(BF16)]
  transfers between devices with their start and end apart: 85 -> 73, of which waited for: 30 -> 26; matrix products, arithmetic and copies ran while one was open for 22% -> 26% of each run, Pallas kernels for 4% -> 5%
where the time goes in v2:
time: 517 us; the launch traced here: 507 us
  waiting for transfers between devices  232 us (45%)
  starting transfers between devices  82.2 us (16%)
  other arithmetic  58.5 us (11%)
  matrix products  52.8 us (10%)
  local copies, waits for them, and re-layouts  42.1 us (8%)
  Pallas kernels  23.5 us (5%)
  between operations  16.2 us (3%)
    ppermute x71, waiting for transfers between devices, swap(): return lax.ppermute(values, axis, [(i, i ^ mask) for i in range(size)])  232 us
    ppermute x71, starting transfers between devices, swap(): return lax.ppermute(values, axis, [(i, i ^ mask) for i in range(size)])  82.2 us
    dot_general x7, matrix products, dot_t(): lax.dot_general(left, right, (((1,), (1,)), ((), ())), preferred_element_...  18.8 us
    pallas_call x1, Pallas kernels, attend_back(): pl.pallas_call(attend_back_kernel, grid=(tokens // MB_TOK,), in_specs=[ro...  14.9 us
    select_n x45, other arithmetic, ordered(): jnp.where(bit == 0, jnp.concatenate([own, peer], axis=axis), jnp.concaten...  14.1 us
    convert_element_type x12, other arithmetic, add(): return (first.astype(F32) + second.astype(F32)).astype(BF16)  13.9 us
    dot_general x7, matrix products, t_dot(): lax.dot_general(left, right, (((0,), (0,)), ((), ())), preferred_element_...  13.4 us
  transfers between devices with their start and end apart: 73, of which 26 were waited for; matrix products, arithmetic and copies ran while one was open for 26% of the time, Pallas kernels for 5%

profile of v2, /device:TPU:1, one launch (start us, length us, event | category | flops | bytes accessed | tf_op | source)
XLA Modules:
  0.0 507.1 jit_solution(14163099635402124377)
XLA Ops:
  21.7 3.4 collective-permute-start.5
  46.8 6.3 %collective-permute-start.27 = (bf16[32,3072]{1,0:T(8,128)(2,1)S(1)}, bf16[32,3072]{1,0:T(8,128)(2,1)S(1)}, u32[]{:S(2)}, u32[]{:S(2)}) collective-permute-start(bf16[32,3072]{1,0:T(8,128)(2,1)S(1)} %get-tuple-element.80), channel_id=1, source_target_pairs={{0,1},{1,0},{2,3},{3,2},{4,5},{5,4},{6,7},{7,6},{8,9},{9,8},{10,11... | collective-permute-start | bytes 589832 | tf_op jit(solution)/shard_map/ppermute | solution.py:78
  53.1 7.0 %collective-permute-done.19 = bf16[128,512]{1,0:T(8,128)(2,1)S(1)} collective-permute-done((bf16[128,512]{1,0:T(8,128)(2,1)S(1)}, bf16[128,512]{1,0:T(8,128)(2,1)S(1)}, u32[]{:S(2)}, u32[]{:S(2)}) %collective-permute-start.19) | collective-permute-done | bytes 131104 | tf_op jit(solution)/shard_map/ppermute | solution.py:78
  67.9 31.6 %collective-permute-done.10 = bf16[64,2048]{1,0:T(8,128)(2,1)S(1)} collective-permute-done((bf16[64,2048]{1,0:T(8,128)(2,1)S(1)}, bf16[64,2048]{1,0:T(8,128)(2,1)S(1)}, u32[]{:S(2)}, u32[]{:S(2)}) %collective-permute-start.10) | collective-permute-done | bytes 262176 | tf_op jit(solution)/shard_map/ppermute | solution.py:78
  109.8 24.9 %collective-permute-done.29 = bf16[64,3072]{1,0:T(8,128)(2,1)S(1)} collective-permute-done((bf16[64,3072]{1,0:T(8,128)(2,1)S(1)}, bf16[64,3072]{1,0:T(8,128)(2,1)S(1)}, u32[]{:S(2)}, u32[]{:S(2)}) %collective-permute-start.29) | collective-permute-done | bytes 393248 | tf_op jit(solution)/shard_map/ppermute | solution.py:78
  137.3 3.5 collective-permute-start.1
  152.4 10.5 %collective-permute-done.33 = bf16[4,64,1536]{2,1,0:T(8,128)(2,1)S(1)} collective-permute-done((bf16[4,64,1536]{2,1,0:T(8,128)(2,1)S(1)}, bf16[4,64,1536]{2,1,0:T(8,128)(2,1)S(1)}, u32[]{:S(2)}, u32[]{:S(2)}) %collective-permute-start.33) | collective-permute-done | bytes 786464 | tf_op jit(solution)/shard_map/ppermute | solution.py:78
  167.9 17.5 %collective-permute-done.13 = bf16[4,2,64,1024]{3,2,1,0:T(8,128)(2,1)S(1)} collective-permute-done((bf16[4,2,64,1024]{3,2,1,0:T(8,128)(2,1)S(1)}, bf16[4,2,64,1024]{3,2,1,0:T(8,128)(2,1)S(1)}, u32[]{:S(2)}, u32[]{:S(2)}) %collective-permute-start.13) | collective-permute-done | bytes 1048608 | tf_op jit(solution)/shard_map/ppermute | solution.py:78
  192.1 8.6 %attend.1 = bf16[512,1024]{1,0:T(8,128)(2,1)} custom-call(f32[512,1024]{1,0:T(8,128)} %fusion.85.q_ref, f32[512,1024]{1,0:T(8,128)} %fusion.84.kv_ref, f32[512,128]{1,0:T(8,128)} %get-tuple-element.113.cos_ref, f32[512,128]{1,0:T(8,128)} %get-tuple-element.114.sin_ref, s32[512,128]{1,0:T(8,128)} %broadcast_in_dim.161.pos_ref, f32[1,128]{1,0:T(1,128)} %reshape.1296.qg_ref, ...), custom_call_target="tpu_custom_call" | custom-call | tf_op jit(solution)/shard_map/attend/pallas_call | solution.py:338
  211.8 6.2 %collective-permute-done.34 = bf16[2,4,64,1536]{3,2,1,0:T(8,128)(2,1)} collective-permute-done((bf16[2,4,64,1536]{3,2,1,0:T(8,128)(2,1)}, bf16[2,4,64,1536]{3,2,1,0:T(8,128)(2,1)}, u32[]{:S(2)}, u32[]{:S(2)}) %collective-permute-start.34) | collective-permute-done | bytes 1572896 | tf_op jit(solution)/shard_map/ppermute | solution.py:78
  220.7 20.8 %collective-permute-done.32 = bf16[4,2,64,1536]{3,2,0,1:T(8,128)(2,1)S(1)} collective-permute-done((bf16[4,2,64,1536]{3,2,0,1:T(8,128)(2,1)S(1)}, bf16[4,2,64,1536]{3,2,0,1:T(8,128)(2,1)S(1)}, u32[]{:S(2)}, u32[]{:S(2)}) %collective-permute-start.32) | collective-permute-done | bytes 1572896 | tf_op jit(solution)/shard_map/ppermute | solution.py:78
  245.0 3.6 fusion.94
  248.6 4.5 fusion.83
  253.3 3.6 multiply_convert_fusion.1
  283.8 5.3 %convolution_convert_fusion = bf16[1536,1024]{1,0:T(8,128)(2,1)} fusion(bf16[512,1536]{1,0:T(8,128)(2,1)S(1)} %get-tuple-element.35, bf16[256,1024]{1,0:T(8,128)(2,1)} %collective-permute-done.36, bf16[256,1024]{1,0:T(8,128)(2,1)} %param.13, pred[]{:T(512)S(6)} %eq.42), kind=kOutput, calls=%fused_computation | convolution fusion | flops 1616904192 | bytes 5767169 | tf_op jit(solution)/shard_map/dot_general | solution.py:230
  289.1 3.4 convolution_convert_fusion.7
  297.1 21.8 %collective-permute-done.55 = bf16[4,2,128,256]{3,2,0,1:T(8,128)(2,1)} collective-permute-done((bf16[4,2,128,256]{3,2,0,1:T(8,128)(2,1)}, bf16[4,2,128,256]{3,2,0,1:T(8,128)(2,1)}, u32[]{:S(2)}, u32[]{:S(2)}) %collective-permute-start.55) | collective-permute-done | bytes 524320 | tf_op jit(solution)/shard_map/ppermute | solution.py:78
  331.3 6.0 %collective-permute-start.60 = (bf16[128,512]{1,0:T(8,128)(2,1)S(1)}, bf16[128,512]{1,0:T(8,128)(2,1)S(1)}, u32[]{:S(2)}, u32[]{:S(2)}) collective-permute-start(bf16[128,512]{1,0:T(8,128)(2,1)S(1)} %get-tuple-element.65), channel_id=1, source_target_pairs={{0,8},{4,12},{8,0},{12,4},{1,9},{5,13},{9,1},{13,5},{2,10},{6,14},... | collective-permute-start | bytes 393224 | tf_op jit(solution)/shard_map/ppermute | solution.py:78
  338.3 11.3 %collective-permute-done.60 = bf16[128,512]{1,0:T(8,128)(2,1)S(1)} collective-permute-done((bf16[128,512]{1,0:T(8,128)(2,1)S(1)}, bf16[128,512]{1,0:T(8,128)(2,1)S(1)}, u32[]{:S(2)}, u32[]{:S(2)}) %collective-permute-start.60) | collective-permute-done | bytes 131104 | tf_op jit(solution)/shard_map/ppermute | solution.py:78
  354.0 14.9 %attend_back.1 = (bf16[512,1024]{1,0:T(8,128)(2,1)}, bf16[512,1024]{1,0:T(8,128)(2,1)}, f32[8,128]{1,0:T(8,128)}, f32[8,128]{1,0:T(8,128)}) custom-call(f32[512,1024]{1,0:T(8,128)} %fusion.85.q_ref, f32[512,1024]{1,0:T(8,128)} %fusion.84.kv_ref, f32[512,128]{1,0:T(8,128)} %get-tuple-element.113.cos_ref, f32[512,128]{1,0:T(8,128)} %get-tuple-element.114.sin_ref, ...), custom_call_target="tpu_custom_call" | custom-call | tf_op jit(solution)/shard_map/attend_back/pallas_call | solution.py:353
  395.8 13.3 %collective-permute-done.42 = f32[4,2,128]{2,1,0:T(2,128)S(1)} collective-permute-done((f32[4,2,128]{2,1,0:T(2,128)S(1)}, f32[4,2,128]{2,1,0:T(2,128)S(1)}, u32[]{:S(2)}, u32[]{:S(2)}) %collective-permute-start.42) | collective-permute-done | bytes 4128 | tf_op jit(solution)/shard_map/ppermute | solution.py:78
  432.4 24.1 %collective-permute-done.68 = bf16[64,3072]{1,0:T(8,128)(2,1)S(1)} collective-permute-done((bf16[64,3072]{1,0:T(8,128)(2,1)S(1)}, bf16[64,3072]{1,0:T(8,128)(2,1)S(1)}, u32[]{:S(2)}, u32[]{:S(2)}) %collective-permute-start.68) | collective-permute-done | bytes 393248 | tf_op jit(solution)/shard_map/ppermute | solution.py:78
  462.6 3.9 collective-permute-start.70
  468.7 14.2 %collective-permute-done.52 = bf16[64,2048]{1,0:T(8,128)(2,1)} collective-permute-done((bf16[64,2048]{1,0:T(8,128)(2,1)}, bf16[64,2048]{1,0:T(8,128)(2,1)}, u32[]{:S(2)}, u32[]{:S(2)}) %collective-permute-start.52) | collective-permute-done | bytes 262176 | tf_op jit(solution)/shard_map/ppermute | solution.py:78
  (464 shorter events, 220.8 us)
Async XLA Ops:
  7.2 241.4 %all-gather.2.cloned.1.call-start = ((), (), s32[]{:S(2)}) async-start(), calls=%async_computation.1 | async-start | bytes 3342336 | tf_op jit(solution)/shard_map/all_gather | solution.py:467
  9.0 33.3 %collective-permute-start.8 = (bf16[32,2048]{1,0:T(8,128)(2,1)S(1)}, bf16[32,2048]{1,0:T(8,128)(2,1)S(1)}, u32[]{:S(2)}, u32[]{:S(2)}) collective-permute-start(bf16[32,2048]{1,0:T(8,128)(2,1)S(1)} %pad_maximum_fusion.7), channel_id=1, source_target_pairs={{0,1},{1,0},{2,3},{3,2},{4,5},{5,4},{6,7},{7,6},{8,9},{9,8},{10,11... | collective-permute-start | bytes 393224 | tf_op jit(solution)/shard_map/ppermute | solution.py:78
  10.4 94.7 %collective-permute-start = (bf16[256,1024]{1,0:T(8,128)(2,1)}, bf16[256,1024]{1,0:T(8,128)(2,1)S(1)}, u32[]{:S(2)}, u32[]{:S(2)}) collective-permute-start(bf16[256,1024]{1,0:T(8,128)(2,1)} %param.12), channel_id=1, source_target_pairs={{0,16},{16,0},{1,17},{17,1},{2,18},{18,2},{3,19},{19,3},{4,20},{20... | collective-permute-start | bytes 1572872 | tf_op jit(solution)/shard_map/ppermute | solution.py:78
  18.0 480.2 %reduce-scatter.2.cloned.1.call-start = ((), (), s32[]{:S(2)}) async-start(), calls=%async_computation.2 | async-start | bytes 3342336 | tf_op jit(solution)/shard_map/reduce_scatter | solution.py:499
  31.2 217.3 %collective-permute-start.36 = (bf16[256,1024]{1,0:T(8,128)(2,1)}, bf16[256,1024]{1,0:T(8,128)(2,1)}, u32[]{:S(2)}, u32[]{:S(2)}) collective-permute-start(bf16[256,1024]{1,0:T(8,128)(2,1)} %param.13), channel_id=1, source_target_pairs={{0,1},{1,0},{2,3},{3,2},{4,5},{5,4},{6,7},{7,6},{8,9},{9,8},{10,11... | collective-permute-start | bytes 1572872 | tf_op jit(solution)/shard_map/ppermute | solution.py:78
  61.2 38.4 %collective-permute-start.10 = (bf16[64,2048]{1,0:T(8,128)(2,1)S(1)}, bf16[64,2048]{1,0:T(8,128)(2,1)S(1)}, u32[]{:S(2)}, u32[]{:S(2)}) collective-permute-start(bf16[64,2048]{1,0:T(8,128)(2,1)S(1)} %maximum_select_fusion.32), channel_id=1, source_target_pairs={{0,8},{4,12},{8,0},{12,4},{1,9},{5,13},{9,1},{13,5},{2,10},{6,14},... | collective-permute-start | bytes 786440 | tf_op jit(solution)/shard_map/ppermute | solution.py:78
  61.6 38.1 %collective-permute-start.9 = (bf16[64,2048]{1,0:T(8,128)(2,1)S(1)}, bf16[64,2048]{1,0:T(8,128)(2,1)S(1)}, u32[]{:S(2)}, u32[]{:S(2)}) collective-permute-start(bf16[64,2048]{1,0:T(8,128)(2,1)S(1)} %maximum_select_fusion.32), channel_id=1, source_target_pairs={{0,4},{4,0},{8,12},{12,8},{1,5},{5,1},{9,13},{13,9},{2,6},{6,2},{1... | collective-permute-start | bytes 786440 | tf_op jit(solution)/shard_map/ppermute | solution.py:78
  67.2 34.6 %collective-permute-start.21 = (bf16[4,128,256]{2,1,0:T(8,128)(2,1)S(1)}, bf16[4,128,256]{2,1,0:T(8,128)(2,1)S(1)}, u32[]{:S(2)}, u32[]{:S(2)}) collective-permute-start(bf16[4,128,256]{2,1,0:T(8,128)(2,1)S(1)} %get-tuple-element.76), channel_id=1, source_target_pairs={{0,2},{2,0},{1,3},{3,1},{4,6},{6,4},{5,7},{7,5},{8,10},{10,8},{9,1... | collective-permute-start | bytes 786440 | tf_op jit(solution)/shard_map/ppermute | solution.py:78
  146.9 56.7 %collective-permute-start.31 = (bf16[4,64,1536]{2,1,0:T(8,128)(2,1)}, bf16[4,64,1536]{2,1,0:T(8,128)(2,1)}, u32[]{:S(2)}, u32[]{:S(2)}) collective-permute-start(bf16[4,64,1536]{2,1,0:T(8,128)(2,1)} %get-tuple-element.48), channel_id=1, source_target_pairs={{0,2},{2,0},{1,3},{3,1},{4,6},{6,4},{5,7},{7,5},{8,10},{10,8},{9,1... | collective-permute-start | bytes 2359304 | tf_op jit(solution)/shard_map/ppermute | solution.py:78
  149.5 35.9 %collective-permute-start.13 = (bf16[4,2,64,1024]{3,2,1,0:T(8,128)(2,1)S(1)}, bf16[4,2,64,1024]{3,2,1,0:T(8,128)(2,1)S(1)}, u32[]{:S(2)}, u32[]{:S(2)}) collective-permute-start(bf16[4,2,64,1024]{3,2,1,0:T(8,128)(2,1)S(1)} %maximum_select_fusion.12), channel_id=1, source_target_pairs={{0,16},{16,0},{1,17},{17,1},{2,18},{18,2},{3,19},{19,3},{4,20},{20... | collective-permute-start | bytes 3145736 | tf_op jit(solution)/shard_map/ppermute | solution.py:78
  164.3 53.7 %collective-permute-start.34 = (bf16[2,4,64,1536]{3,2,1,0:T(8,128)(2,1)}, bf16[2,4,64,1536]{3,2,1,0:T(8,128)(2,1)}, u32[]{:S(2)}, u32[]{:S(2)}) collective-permute-start(bf16[2,4,64,1536]{3,2,1,0:T(8,128)(2,1)} %maximum_select_fusion.9), channel_id=1, source_target_pairs={{0,2},{2,0},{1,3},{3,1},{4,6},{6,4},{5,7},{7,5},{8,10},{10,8},{9,1... | collective-permute-start | bytes 4718600 | tf_op jit(solution)/shard_map/ppermute | solution.py:78
  205.4 36.1 %collective-permute-start.32 = (bf16[4,2,64,1536]{3,2,0,1:T(8,128)(2,1)S(1)}, bf16[4,2,64,1536]{3,2,0,1:T(8,128)(2,1)S(1)}, u32[]{:S(2)}, u32[]{:S(2)}) collective-permute-start(bf16[4,2,64,1536]{3,2,0,1:T(8,128)(2,1)S(1)} %maximum_select_fusion.7), channel_id=1, source_target_pairs={{0,16},{16,0},{1,17},{17,1},{2,18},{18,2},{3,19},{19,3},{4,20},{20... | collective-permute-start | bytes 4718600 | tf_op jit(solution)/shard_map/ppermute | solution.py:78
  268.5 56.7 %collective-permute-start.63 = (bf16[4,2,64,1536]{3,2,1,0:T(8,128)(2,1)}, bf16[4,2,64,1536]{3,2,1,0:T(8,128)(2,1)}, u32[]{:S(2)}, u32[]{:S(2)}) collective-permute-start(bf16[4,2,64,1536]{3,2,1,0:T(8,128)(2,1)} %dynamic-slice_bitcast_fusion.1), channel_id=1, source_target_pairs={{0,16},{16,0},{1,17},{17,1},{2,18},{18,2},{3,19},{19,3},{4,20},{20... | collective-permute-start | bytes 4718600 | tf_op jit(solution)/shard_map/ppermute | solution.py:78
  271.7 57.0 %collective-permute-start.65 = (bf16[2,4,64,1536]{3,2,1,0:T(8,128)(2,1)}, bf16[2,4,64,1536]{3,2,1,0:T(8,128)(2,1)}, u32[]{:S(2)}, u32[]{:S(2)}) collective-permute-start(bf16[2,4,64,1536]{3,2,1,0:T(8,128)(2,1)} %dynamic-slice_bitcast_fusion), channel_id=1, source_target_pairs={{0,2},{2,0},{1,3},{3,1},{4,6},{6,4},{5,7},{7,5},{8,10},{10,8},{9,1... | collective-permute-start | bytes 4718600 | tf_op jit(solution)/shard_map/ppermute | solution.py:78
  282.3 36.6 %collective-permute-start.55 = (bf16[4,2,128,256]{3,2,0,1:T(8,128)(2,1)}, bf16[4,2,128,256]{3,2,0,1:T(8,128)(2,1)}, u32[]{:S(2)}, u32[]{:S(2)}) collective-permute-start(bf16[4,2,128,256]{3,2,0,1:T(8,128)(2,1)} %bitcast.285), channel_id=1, source_target_pairs={{0,16},{16,0},{1,17},{17,1},{2,18},{18,2},{3,19},{19,3},{4,20},{20... | collective-permute-start | bytes 1572872 | tf_op jit(solution)/shard_map/ppermute | solution.py:78
  292.5 58.1 %collective-permute-start.38 = (bf16[512,1024]{1,0:T(8,128)(2,1)}, bf16[512,1024]{1,0:T(8,128)(2,1)}, u32[]{:S(2)}, u32[]{:S(2)}) collective-permute-start(bf16[512,1024]{1,0:T(8,128)(2,1)} %convolution_convert_fusion.7), channel_id=1, source_target_pairs={{0,1},{1,0},{2,3},{3,2},{4,5},{5,4},{6,7},{7,6},{8,9},{9,8},{10,11... | collective-permute-start | bytes 3145736 | tf_op jit(solution)/shard_map/ppermute | solution.py:78
  328.1 58.8 %collective-permute-start.64 = (bf16[4,64,1536]{2,1,0:T(8,128)(2,1)}, bf16[4,64,1536]{2,1,0:T(8,128)(2,1)}, u32[]{:S(2)}, u32[]{:S(2)}) collective-permute-start(bf16[4,64,1536]{2,1,0:T(8,128)(2,1)} %dynamic-slice_bitcast_fusion.5), channel_id=1, source_target_pairs={{0,2},{2,0},{1,3},{3,1},{4,6},{6,4},{5,7},{7,5},{8,10},{10,8},{9,1... | collective-permute-start | bytes 2359304 | tf_op jit(solution)/shard_map/ppermute | solution.py:78
  338.3 50.1 %collective-permute-start.66 = (bf16[4,64,1536]{2,1,0:T(8,128)(2,1)}, bf16[4,64,1536]{2,1,0:T(8,128)(2,1)}, u32[]{:S(2)}, u32[]{:S(2)}) collective-permute-start(bf16[4,64,1536]{2,1,0:T(8,128)(2,1)} %dynamic-slice_bitcast_fusion.4), channel_id=1, source_target_pairs={{0,16},{16,0},{1,17},{17,1},{2,18},{18,2},{3,19},{19,3},{4,20},{20... | collective-permute-start | bytes 2359304 | tf_op jit(solution)/shard_map/ppermute | solution.py:78
  349.7 35.0 %collective-permute-start.62 = (f32[64,512]{1,0:T(8,128)S(1)}, f32[64,512]{1,0:T(8,128)S(1)}, u32[]{:S(2)}, u32[]{:S(2)}) collective-permute-start(f32[64,512]{1,0:T(8,128)S(1)} %get-tuple-element.82), channel_id=1, source_target_pairs={{0,1},{1,0},{2,3},{3,2},{4,5},{5,4},{6,7},{7,6},{8,9},{9,8},{10,11... | collective-permute-start | bytes 393224 | tf_op jit(solution)/shard_map/ppermute | solution.py:78
  381.6 42.3 %collective-permute-start.47 = (bf16[4,2,64,1024]{3,2,1,0:T(8,128)(2,1)}, bf16[4,2,64,1024]{3,2,1,0:T(8,128)(2,1)}, u32[]{:S(2)}, u32[]{:S(2)}) collective-permute-start(bf16[4,2,64,1024]{3,2,1,0:T(8,128)(2,1)} %dynamic-slice_bitcast_fusion.3), channel_id=1, source_target_pairs={{0,16},{16,0},{1,17},{17,1},{2,18},{18,2},{3,19},{19,3},{4,20},{20... | collective-permute-start | bytes 3145736 | tf_op jit(solution)/shard_map/ppermute | solution.py:78
  384.7 41.6 %collective-permute-start.49 = (bf16[2,4,64,1024]{3,2,1,0:T(8,128)(2,1)}, bf16[2,4,64,1024]{3,2,1,0:T(8,128)(2,1)}, u32[]{:S(2)}, u32[]{:S(2)}) collective-permute-start(bf16[2,4,64,1024]{3,2,1,0:T(8,128)(2,1)} %dynamic-slice_bitcast_fusion.2), channel_id=1, source_target_pairs={{0,2},{2,0},{1,3},{3,1},{4,6},{6,4},{5,7},{7,5},{8,10},{10,8},{9,1... | collective-permute-start | bytes 3145736 | tf_op jit(solution)/shard_map/ppermute | solution.py:78
  420.2 36.3 %collective-permute-start.68 = (bf16[64,3072]{1,0:T(8,128)(2,1)S(1)}, bf16[64,3072]{1,0:T(8,128)(2,1)S(1)}, u32[]{:S(2)}, u32[]{:S(2)}) collective-permute-start(bf16[64,3072]{1,0:T(8,128)(2,1)S(1)} %get-tuple-element.41), channel_id=1, source_target_pairs={{0,8},{4,12},{8,0},{12,4},{1,9},{5,13},{9,1},{13,5},{2,10},{6,14},... | collective-permute-start | bytes 1179656 | tf_op jit(solution)/shard_map/ppermute | solution.py:78
  420.2 36.3 %collective-permute-start.67 = (bf16[64,3072]{1,0:T(8,128)(2,1)S(1)}, bf16[64,3072]{1,0:T(8,128)(2,1)S(1)}, u32[]{:S(2)}, u32[]{:S(2)}) collective-permute-start(bf16[64,3072]{1,0:T(8,128)(2,1)S(1)} %get-tuple-element.40), channel_id=1, source_target_pairs={{0,4},{4,0},{8,12},{12,8},{1,5},{5,1},{9,13},{13,9},{2,6},{6,2},{1... | collective-permute-start | bytes 1179656 | tf_op jit(solution)/shard_map/ppermute | solution.py:78
  423.9 62.0 %collective-permute-start.40 = (bf16[256,1024]{1,0:T(8,128)(2,1)S(1)}, bf16[256,1024]{1,0:T(8,128)(2,1)}, u32[]{:S(2)}, u32[]{:S(2)}) collective-permute-start(bf16[256,1024]{1,0:T(8,128)(2,1)S(1)} %add_convert_fusion.1), channel_id=1, source_target_pairs={{0,16},{16,0},{1,17},{17,1},{2,18},{18,2},{3,19},{19,3},{4,20},{20... | collective-permute-start | bytes 1572872 | tf_op jit(solution)/shard_map/ppermute | solution.py:78
  (113 other events, 1451.4 us)
Sparse Core Ops, SparseCore 0:
  18.1 85.5 all-gather.1
  289.2 155.1 reduce-scatter.1
